TPU v7x, 128 devices: a whole 4x4x4 slice. The times are simulated.
128 devices in a mesh: grp: 8 (over x, core), exp: 16 (over z, y).
Axes of the slice: x: 4, y: 4, z: 4, core: 2. Of those that a mesh axis runs over, the one named last changes fastest.
Arguments:
- tokens: bfloat16 [16384, 4096], P(('grp', 'exp')), may hold values from -6 to 6
- expert_ids: int32 [16384, 8], P(('grp', 'exp')), may hold values from 0 to 15, all different within a row; in each aligned block of 128 rows (0 to 127, 128 to 255, ...) at most 80 rows name the same one
- gate_fixed: int32 [16384, 8], P(('grp', 'exp')), may hold values from 1 to 65535
- w_gate: bfloat16 [16, 4096, 768], P('exp', None, 'grp'), may hold values from -0.09375 to 0.09375
- w_up: bfloat16 [16, 4096, 768], P('exp', None, 'grp'), may hold values from -0.09375 to 0.09375
- w_down: bfloat16 [16, 768, 4096], P('exp', 'grp'), may hold values from -0.21875 to 0.21875
Outputs:
- mixed: bfloat16 [16384, 4096], P(('grp', 'exp'))
Inputs may be any that keep to these rules, and one draw needn't show every extreme that they name: `expert_ids`: each row names 8 different experts. Among the rows of one device no expert is named by more than 80 rows, and in every draw some expert is named by exactly 80 rows of some device.
All inputs are finite; a program needn't handle non-finite values.
Results may differ from a plain program's by a relative error of at most 0.0058.
Values may be sent and summed in bfloat16 or wider, within the bound.
No kernel may reach another device: no remote copies, remote signals or barrier semaphores. Data moves between devices by JAX's collectives and lax.ppermute only.
A program may use at most 128 MiB of HBM per device.

v0:
```python
import functools

import jax
import jax.numpy as jnp
from jax import lax
from jax.experimental import pallas as pl
from jax.experimental.pallas import tpu as pltpu
from jax.sharding import PartitionSpec as P


EXPERTS = 16
CAP = 80
NTILE = 256
CTILE = 512


TREE = {
    (1, 0): [(0, 128, (1, 0), (0, 0))],
    (-1, 0): [(0, 128, (-1, 0), (0, 0))],
    (0, 1): [(0, 128, (0, 1), (0, 0))],
    (0, -1): [(0, 128, (0, -1), (0, 0))],
    (-1, -1): [(0, 128, (-1, 0), (0, -1))],
    (1, -1): [(0, 128, (0, -1), (1, 0))],
    (-1, 1): [(0, 128, (0, 1), (-1, 0))],
    (1, 1): [(0, 128, (1, 0), (0, 1))],
    (2, -1): [(0, 128, (-1, 0), (-1, -1))],
    (-1, 2): [(0, 128, (0, -1), (-1, -1))],
    (0, 2): [(0, 128, (0, 1), (0, 1))],
    (2, 0): [(0, 128, (1, 0), (1, 0))],
    (2, 2): [(0, 64, (0, -1), (2, -1)), (64, 64, (-1, 0), (-1, 2))],
    (1, 2): [(0, 128, (0, 1), (1, 1))],
    (2, 1): [(0, 128, (1, 0), (1, 1))],
}

BATCHES = [
    [(2, 2), (2, 1), (1, 2)],
    [(2, -1), (-1, 2), (2, 0), (0, 2)],
    [(-1, -1), (1, 1), (1, -1), (-1, 1)],
    [(0, 0), (1, 0), (-1, 0), (0, 1), (0, -1)],
]


def get_exp(x, dz, dy):
    pairs = [
        (((z + dz) % 4) * 4 + (y + dy) % 4, z * 4 + y) for z in range(4) for y in range(4)
    ]
    return lax.ppermute(x, "exp", pairs)


def get_x(v, dx):
    pairs = [(((x + dx) % 4) * 2 + c, x * 2 + c) for x in range(4) for c in range(2)]
    return lax.ppermute(v, "grp", pairs)


def get_core(v):
    pairs = [(x * 2 + 1 - c, x * 2 + c) for x in range(4) for c in range(2)]
    return lax.ppermute(v, "grp", pairs)


def gather_weights(w):
    half = w.shape[0] // 2
    right = get_x(w, 1)
    left = get_x(w, -1)
    far_a = get_x(right[:half], 1)
    far_b = get_x(left[half:], -1)
    mine = [w, right, left, far_a, far_b]
    other = []
    for v in mine:
        other.append(get_core(v))
    return mine + other


def gather_tokens(t):
    blocks = {(0, 0): [t]}
    for offset, parts in TREE.items():
        blocks[offset] = []
        for row, rows, way, before in parts:
            (source,) = blocks[before]
            if rows < source.shape[0]:
                source = source[row : row + rows]
            blocks[offset].append(get_exp(source, *way))
    return blocks


def add_up(value, extra):
    rows = value.shape[0]
    cuts = sorted({0, rows} | {r for r, _ in extra} | {r + v.shape[0] for r, v in extra})
    pieces = []
    for lo, hi in zip(cuts, cuts[1:]):
        total = value[lo:hi].astype(jnp.float32)
        for row, v in extra:
            if row <= lo and hi <= row + v.shape[0]:
                total = total + v[lo - row : hi - row].astype(jnp.float32)
        pieces.append(total.astype(jnp.bfloat16))
    return pieces[0] if len(pieces) == 1 else jnp.concatenate(pieces, axis=0)


def reduce_back(partial):
    extra = {offset: [] for offset in partial}
    for offset, parts in reversed(TREE.items()):
        values = partial[offset]
        if extra[offset]:
            values = [add_up(values[0], extra[offset])]
        for i, (row, rows, way, before) in enumerate(parts):
            extra[before].append((row, get_exp(values[i], -way[0], -way[1])))
    return add_up(partial[0, 0][0], extra[0, 0])


def weight_pieces(n):
    half = 3 * n // 2
    pieces = []

    def cut(operand, row, kind, to, count):
        while count:
            part = min(count, NTILE - to % NTILE)
            pieces.append((operand, row, kind, to, part))
            row, to, count = row + part, to + part, count - part

    for core in range(2):
        for k in range(3):
            for kind in range(3):
                cut(core * 5 + k, kind * n, kind, (core * 4 + k) * n, n)
        for kind in range(3):
            lo, hi = kind * n, (kind + 1) * n
            base = (core * 4 + 3) * n
            for operand, start in ((3, 0), (4, half)):
                a, b = max(lo, start), min(hi, start + half)
                if a < b:
                    cut(core * 5 + operand, a - start, kind, base + a - lo, b - a)
    pieces.sort(key=lambda p: (p[2] == 2, p[3]))
    return pieces


def expert_body(nb, parts, pieces, src_ref, meta_ref, *refs):
    np_ = len(parts)
    inputs, weights, outs = refs[:np_], refs[np_ : np_ + 10], refs[np_ + 10 : 2 * np_ + 10]
    w_ref, t_ref, x_ref, h_ref, o_ref, p_ref, s_ref, k_ref, t_sem, w_sem, o_sem = refs[2 * np_ + 10 :]
    hidden = w_ref.shape[1]
    width = w_ref.shape[2]
    tiles = hidden // NTILE

    for i, (b, row, rows) in enumerate(parts):
        pltpu.make_async_copy(inputs[i], t_ref.at[b, pl.ds(row, rows)], t_sem.at[b]).start()

    def fetch(stage):
        for operand, row, kind, to, count in pieces:
            if (tiles if kind == 2 else to // NTILE) == stage:
                pltpu.make_async_copy(
                    weights[operand].at[pl.ds(row, count)],
                    w_ref.at[kind, pl.ds(to, count)],
                    w_sem.at[stage],
                ).start()

    fetch(0)

    def out_copy(i):
        b, row, rows = parts[i]
        return pltpu.make_async_copy(p_ref.at[b, pl.ds(row, rows)], outs[i], o_sem.at[i])

    slots = lax.broadcasted_iota(jnp.int32, (CAP, 128), 0).astype(jnp.float32) + 1.0

    @pl.loop(0, nb)
    def _(b):
        source = src_ref[b]
        hit = jnp.where(slots == meta_ref[source, 0:1, :], 1.0, 0.0)
        scale = jnp.sum(hit * meta_ref[source, 1:2, :], axis=1, keepdims=True)
        rows = pl.ds(pl.multiple_of(b * CAP, CAP), CAP)
        k_ref[rows, :] = jnp.broadcast_to(scale, (CAP, 128))
        s_ref[b] = hit.T.astype(jnp.bfloat16)
        pltpu.make_async_copy(t_ref.at[b], t_ref.at[b], t_sem.at[b]).wait()
        x_ref[rows, :] = jnp.dot(
            hit.astype(jnp.bfloat16), t_ref[b], preferred_element_type=jnp.float32
        ).astype(jnp.bfloat16)

    fetch(1)

    nt = (((1,), (1,)), ((), ()))

    @pl.loop(0, tiles)
    def _(n):
        rows = pl.ds(pl.multiple_of(n * NTILE, NTILE), NTILE)
        both = w_ref.at[pl.ds(0, 2), rows]
        pltpu.make_async_copy(both, both, w_sem.at[n]).wait()
        for stage in range(2, tiles + 1):

            @pl.when(n == stage - 2)
            def _():
                fetch(stage)

        gate = lax.dot_general(x_ref[...], w_ref[0, rows, :], nt, preferred_element_type=jnp.float32)
        up = lax.dot_general(x_ref[...], w_ref[1, rows, :], nt, preferred_element_type=jnp.float32)
        h_ref[:, rows] = (gate / (1.0 + jnp.exp(-gate)) * up).astype(jnp.bfloat16)

    pltpu.make_async_copy(w_ref.at[2], w_ref.at[2], w_sem.at[tiles]).wait()

    @pl.loop(0, width // CTILE)
    def _(c):
        cols = pl.ds(pl.multiple_of(c * CTILE, CTILE), CTILE)
        out = jnp.dot(h_ref[...], w_ref[2, :, cols], preferred_element_type=jnp.float32)
        o_ref[:, cols] = (out * jnp.tile(k_ref[...], (1, CTILE // 128))).astype(jnp.bfloat16)

    for b in range(nb):
        p_ref[b] = jnp.dot(
            s_ref[b], o_ref[b * CAP : (b + 1) * CAP, :], preferred_element_type=jnp.float32
        ).astype(jnp.bfloat16)
        for i, (block, row, rows) in enumerate(parts):
            if block == b:
                out_copy(i).start()
    for i in range(np_):
        out_copy(i).wait()


def expert_blocks(src, meta, blocks, weights):
    nb = len(blocks)
    parts, inputs = [], []
    for b, block in enumerate(blocks):
        row = 0
        for part in block:
            parts.append((b, row, part.shape[0]))
            inputs.append(part)
            row += part.shape[0]
    rows, width = row, inputs[0].shape[1]
    n = weights[0].shape[0] // 3
    hidden = 8 * n
    pieces = weight_pieces(n)
    m = nb * CAP
    anywhere = pl.BlockSpec(memory_space=pl.ANY)
    flops = 2 * m * width * hidden * 3 + 4 * m * rows * width
    moved = 2 * (3 * hidden * width + 2 * nb * rows * width)
    outs = pl.pallas_call(
        functools.partial(expert_body, nb, parts, pieces),
        out_shape=[jax.ShapeDtypeStruct(v.shape, jnp.bfloat16) for v in inputs],
        in_specs=[
            pl.BlockSpec(memory_space=pltpu.SMEM),
            pl.BlockSpec(memory_space=pltpu.VMEM),
        ]
        + [anywhere] * (len(parts) + 10),
        out_specs=[anywhere] * len(parts),
        scratch_shapes=[
            pltpu.VMEM((3, hidden, width), jnp.bfloat16),
            pltpu.VMEM((nb, rows, width), jnp.bfloat16),
            pltpu.VMEM((m, width), jnp.bfloat16),
            pltpu.VMEM((m, hidden), jnp.bfloat16),
            pltpu.VMEM((m, width), jnp.bfloat16),
            pltpu.VMEM((nb, rows, width), jnp.bfloat16),
            pltpu.VMEM((nb, rows, CAP), jnp.bfloat16),
            pltpu.VMEM((m, 128), jnp.float32),
            pltpu.SemaphoreType.DMA((nb,)),
            pltpu.SemaphoreType.DMA((hidden // NTILE + 1,)),
            pltpu.SemaphoreType.DMA((len(parts),)),
        ],
        compiler_params=pltpu.CompilerParams(vmem_limit_bytes=50 << 20),
        cost_estimate=pl.CostEstimate(flops=flops, bytes_accessed=moved, transcendentals=m * hidden),
    )(src, meta, *inputs, *weights)
    return [[v for v, part in zip(outs, parts) if part[0] == b] for b in range(nb)]


def per_device(tokens, expert_ids, gate_fixed, w_gate, w_up, w_down):
    me = lax.axis_index("exp")
    blocks = gather_tokens(tokens)
    weights = gather_weights(jnp.concatenate([w_gate[0].T, w_up[0].T, w_down[0]], axis=0))

    hit = expert_ids.T[None] == jnp.arange(EXPERTS, dtype=jnp.int32)[:, None, None]
    routed = jnp.any(hit, axis=1).astype(jnp.int32)
    place = jnp.cumsum(routed, axis=1) * routed
    gate = jnp.sum(jnp.where(hit, gate_fixed.T[None], 0), axis=1)
    meta = jnp.stack([place.astype(jnp.float32), gate.astype(jnp.float32) / 65536.0], axis=1)
    meta = lax.all_to_all(meta, "exp", split_axis=0, concat_axis=0, tiled=True)

    partial = {}
    for batch in BATCHES:
        dz = jnp.array([o[0] for o in batch], jnp.int32)
        dy = jnp.array([o[1] for o in batch], jnp.int32)
        src = (((me >> 2) + dz) & 3) * 4 + ((me + dy) & 3)
        outs = expert_blocks(src, meta, [blocks[o] for o in batch], weights)
        partial.update(zip(batch, outs))
    return reduce_back(partial)


def solution(mesh):
    in_specs = (
        P(("grp", "exp"), None),
        P(("grp", "exp"), None),
        P(("grp", "exp"), None),
        P("exp", None, "grp"),
        P("exp", None, "grp"),
        P("exp", "grp", None),
    )
    out_specs = P(("grp", "exp"), None)

    return jax.shard_map(
        per_device, mesh=mesh, in_specs=in_specs, out_specs=out_specs, check_vma=False
    )
```

profile of v0, /device:TPU:2, one launch (start us, length us, event | category | flops | bytes accessed | tf_op | source)
XLA Modules:
  0.0 331.8 jit_solution(11336466691185360521)
XLA Ops:
  3.2 1.9 pad_maximum_fusion.refs_5_.refs_4_
  5.7 4.1 %collective-permute-start = (bf16[128,4096]{1,0:T(8,128)(2,1)S(1)}, bf16[128,4096]{1,0:T(8,128)(2,1)}, u32[]{:S(2)}, u32[]{:S(2)}) collective-permute-start(bf16[128,4096]{1,0:T(8,128)(2,1)S(1)} %copy-done.18), channel_id=1, source_target_pairs={{4,0},{5,1},{6,2},{7,3},{8,4},{9,5},{10,6},{11,7},{12,8},{13,9},{1... | collective-permute-start | bytes 3145736 | tf_op jit(solution)/shard_map/ppermute | solution.py:47
  9.9 16.5 %collective-permute-done.3.refs_4_ = bf16[128,4096]{1,0:T(8,128)(2,1)S(1)} collective-permute-done((bf16[128,4096]{1,0:T(8,128)(2,1)}, bf16[128,4096]{1,0:T(8,128)(2,1)S(1)}, u32[]{:S(2)}, u32[]{:S(2)}) %collective-permute-start.3) | collective-permute-done | bytes 1048608 | tf_op jit(solution)/shard_map/ppermute | solution.py:47
  27.9 3.6 %collective-permute-done.refs_1_ = bf16[128,4096]{1,0:T(8,128)(2,1)} collective-permute-done((bf16[128,4096]{1,0:T(8,128)(2,1)S(1)}, bf16[128,4096]{1,0:T(8,128)(2,1)}, u32[]{:S(2)}, u32[]{:S(2)}) %collective-permute-start) | collective-permute-done | bytes 1048608 | tf_op jit(solution)/shard_map/ppermute | solution.py:47
  32.1 3.3 %collective-permute-done.1.refs_2_ = bf16[128,4096]{1,0:T(8,128)(2,1)S(1)} collective-permute-done((bf16[128,4096]{1,0:T(8,128)(2,1)S(1)}, bf16[128,4096]{1,0:T(8,128)(2,1)S(1)}, u32[]{:S(2)}, u32[]{:S(2)}) %collective-permute-start.1) | collective-permute-done | bytes 1048608 | tf_op jit(solution)/shard_map/ppermute | solution.py:47
  36.5 20.9 %collective-permute-done.13.refs_0_ = bf16[128,4096]{1,0:T(8,128)(2,1)S(1)} collective-permute-done((bf16[128,4096]{1,0:T(8,128)(2,1)S(1)}, bf16[128,4096]{1,0:T(8,128)(2,1)S(1)}, u32[]{:S(2)}, u32[]{:S(2)}) %collective-permute-start.13) | collective-permute-done | bytes 1048608 | tf_op jit(solution)/shard_map/ppermute | solution.py:47
  58.1 3.7 %collective-permute-start.23 = (bf16[128,4096]{1,0:T(8,128)(2,1)S(1)}, bf16[128,4096]{1,0:T(8,128)(2,1)S(1)}, u32[]{:S(2)}, u32[]{:S(2)}) collective-permute-start(bf16[128,4096]{1,0:T(8,128)(2,1)S(1)} %collective-permute-done.14.refs_1_), channel_id=1, source_target_pairs={{4,0},{5,1},{6,2},{7,3},{8,4},{9,5},{10,6},{11,7},{12,8},{13,9},{1... | collective-permute-start | bytes 3145736 | tf_op jit(solution)/shard_map/ppermute | solution.py:47
  62.0 16.7 %collective-permute-done.5.refs_7_.refs_6_ = bf16[288,4096]{1,0:T(8,128)(2,1)} collective-permute-done((bf16[288,4096]{1,0:T(8,128)(2,1)S(1)}, bf16[288,4096]{1,0:T(8,128)(2,1)}, u32[]{:S(2)}, u32[]{:S(2)}) %collective-permute-start.5) | collective-permute-done | bytes 2359328 | tf_op jit(solution)/shard_map/ppermute | solution.py:52
  78.7 1.9 collective-permute-start.6
  82.2 2.4 slice.33
  85.6 19.3 %collective-permute-done.6.refs_8_.refs_7_ = bf16[144,4096]{1,0:T(8,128)(2,1)} collective-permute-done((bf16[144,4096]{1,0:T(8,128)(2,1)S(1)}, bf16[144,4096]{1,0:T(8,128)(2,1)}, u32[]{:S(2)}, u32[]{:S(2)}) %collective-permute-start.6) | collective-permute-done | bytes 1179680 | tf_op jit(solution)/shard_map/ppermute | solution.py:52
  107.1 1.9 slice.35
  110.6 1.9 collective-permute-start.22
  112.5 9.1 %collective-permute-done.21.refs_0_ = bf16[64,4096]{1,0:T(8,128)(2,1)S(1)} collective-permute-done((bf16[64,4096]{1,0:T(8,128)(2,1)}, bf16[64,4096]{1,0:T(8,128)(2,1)S(1)}, u32[]{:S(2)}, u32[]{:S(2)}) %collective-permute-start.21) | collective-permute-done | bytes 524320 | tf_op jit(solution)/shard_map/ppermute | solution.py:47
  122.2 5.7 %all-to-all-start = ((f32[16,2,128]{2,1,0:T(2,128)}), f32[16,2,128]{2,1,0:T(2,128)S(1)}, u32[]{:S(2)}, u32[]{:S(2)}) async-start(f32[16,2,128]{2,1,0:T(2,128)} %pad_maximum_fusion.3), calls=%async_computation | async-start | bytes 32768 | tf_op jit(solution)/shard_map/all_to_all | solution.py:268
  127.9 3.2 collective-permute-start.20
  131.1 2.7 collective-permute-start.19
  134.0 3.2 collective-permute-start.16
  137.2 14.0 %shard_map.139 = (bf16[64,4096]{1,0:T(8,128)(2,1)S(1)}, bf16[64,4096]{1,0:T(8,128)(2,1)S(1)}, bf16[128,4096]{1,0:T(8,128)(2,1)S(1)}, bf16[128,4096]{1,0:T(8,128)(2,1)}) custom-call(s32[3]{0:T(128)S(1)} %and_add_fusion.src_ref, f32[16,2,128]{2,1,0:T(2,128)S(1)} %all-to-all-done.meta_ref, bf16[64,4096]{1,0:T(8,128)(2,1)S(1)} %collective-permute-done.21.refs_0_, ...), custom_call_target="tpu_custom_call" | custom-call | flops 5033164800 | bytes 25165824 | tf_op jit(solution)/shard_map/pallas_call | solution.py:230
  152.2 5.5 %collective-permute-done.19.refs_2_ = bf16[128,4096]{1,0:T(8,128)(2,1)} collective-permute-done((bf16[128,4096]{1,0:T(8,128)(2,1)}, bf16[128,4096]{1,0:T(8,128)(2,1)}, u32[]{:S(2)}, u32[]{:S(2)}) %collective-permute-start.19) | collective-permute-done | bytes 1048608 | tf_op jit(solution)/shard_map/ppermute | solution.py:47
  157.7 16.0 %shard_map.138 = (bf16[128,4096]{1,0:T(8,128)(2,1)S(1)}, bf16[128,4096]{1,0:T(8,128)(2,1)S(1)}, bf16[128,4096]{1,0:T(8,128)(2,1)S(1)}, bf16[128,4096]{1,0:T(8,128)(2,1)}) custom-call(s32[4]{0:T(128)S(1)} %and_add_fusion.1.src_ref, f32[16,2,128]{2,1,0:T(2,128)S(1)} %all-to-all-done.meta_ref, bf16[128,4096]{1,0:T(8,128)(2,1)} %copy-done.7, ...), custom_call_target="tpu_custom_call" | custom-call | flops 6710886400 | bytes 27262976 | tf_op jit(solution)/shard_map/pallas_call | solution.py:230
  176.4 18.0 %shard_map.136 = (bf16[128,4096]{1,0:T(8,128)(2,1)S(1)}, bf16[128,4096]{1,0:T(8,128)(2,1)S(1)}, bf16[128,4096]{1,0:T(8,128)(2,1)S(1)}, bf16[128,4096]{1,0:T(8,128)(2,1)}, bf16[128,4096]{1,0:T(8,128)(2,1)}) custom-call(s32[5]{0:T(128)S(1)} %and_add_fusion.3.src_ref, f32[16,2,128]{2,1,0:T(2,128)S(1)} %all-to-all-done.meta_ref, bf16[128,4096]{1,0:T(8,128)(2,1)} %refs_0_.1, ...), custom_call_target="tpu_custom_call" | custom-call | flops 8388608000 | bytes 29360128 | tf_op jit(solution)/shard_map/pallas_call | solution.py:230
  195.6 16.0 %shard_map.137 = (bf16[128,4096]{1,0:T(8,128)(2,1)S(1)}, bf16[128,4096]{1,0:T(8,128)(2,1)S(1)}, bf16[128,4096]{1,0:T(8,128)(2,1)S(1)}, bf16[128,4096]{1,0:T(8,128)(2,1)}) custom-call(s32[4]{0:T(128)S(1)} %and_add_fusion.2.src_ref, f32[16,2,128]{2,1,0:T(2,128)S(1)} %all-to-all-done.meta_ref, bf16[128,4096]{1,0:T(8,128)(2,1)} %copy-done.22, ...), custom_call_target="tpu_custom_call" | custom-call | flops 6710886400 | bytes 27262976 | tf_op jit(solution)/shard_map/pallas_call | solution.py:230
  215.2 2.8 collective-permute-start.26
  218.0 4.0 %collective-permute-done.33 = bf16[128,4096]{1,0:T(8,128)(2,1)} collective-permute-done((bf16[128,4096]{1,0:T(8,128)(2,1)}, bf16[128,4096]{1,0:T(8,128)(2,1)}, u32[]{:S(2)}, u32[]{:S(2)}) %collective-permute-start.33) | collective-permute-done | bytes 1048608 | tf_op jit(solution)/shard_map/ppermute | solution.py:47
  222.0 2.1 collective-permute-start.28
  224.1 2.0 add_convert_fusion.4
  226.1 37.2 %collective-permute-done.36 = bf16[128,4096]{1,0:T(8,128)(2,1)S(1)} collective-permute-done((bf16[128,4096]{1,0:T(8,128)(2,1)}, bf16[128,4096]{1,0:T(8,128)(2,1)S(1)}, u32[]{:S(2)}, u32[]{:S(2)}) %collective-permute-start.36) | collective-permute-done | bytes 1048608 | tf_op jit(solution)/shard_map/ppermute | solution.py:47
  268.1 17.0 %collective-permute-done.39 = bf16[128,4096]{1,0:T(8,128)(2,1)S(1)} collective-permute-done((bf16[128,4096]{1,0:T(8,128)(2,1)S(1)}, bf16[128,4096]{1,0:T(8,128)(2,1)S(1)}, u32[]{:S(2)}, u32[]{:S(2)}) %collective-permute-start.39) | collective-permute-done | bytes 1048608 | tf_op jit(solution)/shard_map/ppermute | solution.py:47
  288.5 4.0 %collective-permute-start.35 = (bf16[128,4096]{1,0:T(8,128)(2,1)S(1)}, bf16[128,4096]{1,0:T(8,128)(2,1)S(1)}, u32[]{:S(2)}, u32[]{:S(2)}) collective-permute-start(bf16[128,4096]{1,0:T(8,128)(2,1)S(1)} %add_convert_fusion.3), channel_id=1, source_target_pairs={{3,0},{0,1},{1,2},{2,3},{7,4},{4,5},{5,6},{6,7},{11,8},{8,9},{9,10... | collective-permute-start | bytes 3145736 | tf_op jit(solution)/shard_map/ppermute | solution.py:47
  292.5 16.5 %collective-permute-done.29 = bf16[128,4096]{1,0:T(8,128)(2,1)S(1)} collective-permute-done((bf16[128,4096]{1,0:T(8,128)(2,1)S(1)}, bf16[128,4096]{1,0:T(8,128)(2,1)S(1)}, u32[]{:S(2)}, u32[]{:S(2)}) %collective-permute-start.29) | collective-permute-done | bytes 1048608 | tf_op jit(solution)/shard_map/ppermute | solution.py:47
  309.5 20.5 %collective-permute-done.30 = bf16[128,4096]{1,0:T(8,128)(2,1)S(1)} collective-permute-done((bf16[128,4096]{1,0:T(8,128)(2,1)S(1)}, bf16[128,4096]{1,0:T(8,128)(2,1)S(1)}, u32[]{:S(2)}, u32[]{:S(2)}) %collective-permute-start.30) | collective-permute-done | bytes 1048608 | tf_op jit(solution)/shard_map/ppermute | solution.py:47
  (133 shorter events, 33.6 us)
Async XLA Ops:
  0.0 26.4 %collective-permute-start.3 = (bf16[128,4096]{1,0:T(8,128)(2,1)}, bf16[128,4096]{1,0:T(8,128)(2,1)S(1)}, u32[]{:S(2)}, u32[]{:S(2)}) collective-permute-start(bf16[128,4096]{1,0:T(8,128)(2,1)} %refs_0_.1), channel_id=1, source_target_pairs={{3,0},{0,1},{1,2},{2,3},{7,4},{4,5},{5,6},{6,7},{11,8},{8,9},{9,10... | collective-permute-start | bytes 3145736 | tf_op jit(solution)/shard_map/ppermute | solution.py:47
  1.6 26.3 %collective-permute-start.2 = (bf16[128,4096]{1,0:T(8,128)(2,1)}, bf16[128,4096]{1,0:T(8,128)(2,1)S(1)}, u32[]{:S(2)}, u32[]{:S(2)}) collective-permute-start(bf16[128,4096]{1,0:T(8,128)(2,1)} %refs_0_.1), channel_id=1, source_target_pairs={{1,0},{2,1},{3,2},{0,3},{5,4},{6,5},{7,6},{4,7},{9,8},{10,9},{11,1... | collective-permute-start | bytes 3145736 | tf_op jit(solution)/shard_map/ppermute | solution.py:47
  5.2 52.9 %collective-permute-start.4 = (bf16[288,4096]{1,0:T(8,128)(2,1)S(1)}, bf16[288,4096]{1,0:T(8,128)(2,1)S(1)}, u32[]{:S(2)}, u32[]{:S(2)}) collective-permute-start(bf16[288,4096]{1,0:T(8,128)(2,1)S(1)} %pad_maximum_fusion.refs_5_.refs_4_), channel_id=1, source_target_pairs={{32,0},{48,16},{64,32},{80,48},{96,64},{112,80},{0,96},{16,112},{3... | collective-permute-start | bytes 7077896 | tf_op jit(solution)/shard_map/ppermute | solution.py:52
  5.7 25.8 %collective-permute-start = (bf16[128,4096]{1,0:T(8,128)(2,1)S(1)}, bf16[128,4096]{1,0:T(8,128)(2,1)}, u32[]{:S(2)}, u32[]{:S(2)}) collective-permute-start(bf16[128,4096]{1,0:T(8,128)(2,1)S(1)} %copy-done.18), channel_id=1, source_target_pairs={{4,0},{5,1},{6,2},{7,3},{8,4},{9,5},{10,6},{11,7},{12,8},{13,9},{1... | collective-permute-start | bytes 3145736 | tf_op jit(solution)/shard_map/ppermute | solution.py:47
  9.9 25.6 %collective-permute-start.1 = (bf16[128,4096]{1,0:T(8,128)(2,1)S(1)}, bf16[128,4096]{1,0:T(8,128)(2,1)S(1)}, u32[]{:S(2)}, u32[]{:S(2)}) collective-permute-start(bf16[128,4096]{1,0:T(8,128)(2,1)S(1)} %copy-done.18), channel_id=1, source_target_pairs={{12,0},{13,1},{14,2},{15,3},{0,4},{1,5},{2,6},{3,7},{4,8},{5,9},{6... | collective-permute-start | bytes 3145736 | tf_op jit(solution)/shard_map/ppermute | solution.py:47
  26.4 52.3 %collective-permute-start.5 = (bf16[288,4096]{1,0:T(8,128)(2,1)S(1)}, bf16[288,4096]{1,0:T(8,128)(2,1)}, u32[]{:S(2)}, u32[]{:S(2)}) collective-permute-start(bf16[288,4096]{1,0:T(8,128)(2,1)S(1)} %pad_maximum_fusion.refs_5_.refs_4_), channel_id=1, source_target_pairs={{96,0},{112,16},{0,32},{16,48},{32,64},{48,80},{64,96},{80,112},{9... | collective-permute-start | bytes 7077896 | tf_op jit(solution)/shard_map/ppermute | solution.py:52
  27.9 52.7 %collective-permute-start.8 = (bf16[288,4096]{1,0:T(8,128)(2,1)S(1)}, bf16[288,4096]{1,0:T(8,128)(2,1)S(1)}, u32[]{:S(2)}, u32[]{:S(2)}) collective-permute-start(bf16[288,4096]{1,0:T(8,128)(2,1)S(1)} %pad_maximum_fusion.refs_5_.refs_4_), channel_id=1, source_target_pairs={{16,0},{0,16},{48,32},{32,48},{80,64},{64,80},{112,96},{96,112},{1... | collective-permute-start | bytes 7077896 | tf_op jit(solution)/shard_map/ppermute | solution.py:57
  31.5 25.9 %collective-permute-start.13 = (bf16[128,4096]{1,0:T(8,128)(2,1)S(1)}, bf16[128,4096]{1,0:T(8,128)(2,1)S(1)}, u32[]{:S(2)}, u32[]{:S(2)}) collective-permute-start(bf16[128,4096]{1,0:T(8,128)(2,1)S(1)} %collective-permute-done.3.refs_4_), channel_id=1, source_target_pairs={{12,0},{13,1},{14,2},{15,3},{0,4},{1,5},{2,6},{3,7},{4,8},{5,9},{6... | collective-permute-start | bytes 3145736 | tf_op jit(solution)/shard_map/ppermute | solution.py:47
  57.4 27.3 %collective-permute-start.17 = (bf16[128,4096]{1,0:T(8,128)(2,1)S(1)}, bf16[128,4096]{1,0:T(8,128)(2,1)S(1)}, u32[]{:S(2)}, u32[]{:S(2)}) collective-permute-start(bf16[128,4096]{1,0:T(8,128)(2,1)S(1)} %collective-permute-done.13.refs_0_), channel_id=1, source_target_pairs={{12,0},{13,1},{14,2},{15,3},{0,4},{1,5},{2,6},{3,7},{4,8},{5,9},{6... | collective-permute-start | bytes 3145736 | tf_op jit(solution)/shard_map/ppermute | solution.py:47
  57.9 27.1 %collective-permute-start.18 = (bf16[128,4096]{1,0:T(8,128)(2,1)S(1)}, bf16[128,4096]{1,0:T(8,128)(2,1)}, u32[]{:S(2)}, u32[]{:S(2)}) collective-permute-start(bf16[128,4096]{1,0:T(8,128)(2,1)S(1)} %collective-permute-done.13.refs_0_), channel_id=1, source_target_pairs={{3,0},{0,1},{1,2},{2,3},{7,4},{4,5},{5,6},{6,7},{11,8},{8,9},{9,10... | collective-permute-start | bytes 3145736 | tf_op jit(solution)/shard_map/ppermute | solution.py:47
  58.1 26.9 %collective-permute-start.23 = (bf16[128,4096]{1,0:T(8,128)(2,1)S(1)}, bf16[128,4096]{1,0:T(8,128)(2,1)S(1)}, u32[]{:S(2)}, u32[]{:S(2)}) collective-permute-start(bf16[128,4096]{1,0:T(8,128)(2,1)S(1)} %collective-permute-done.14.refs_1_), channel_id=1, source_target_pairs={{4,0},{5,1},{6,2},{7,3},{8,4},{9,5},{10,6},{11,7},{12,8},{13,9},{1... | collective-permute-start | bytes 3145736 | tf_op jit(solution)/shard_map/ppermute | solution.py:47
  78.7 26.2 %collective-permute-start.6 = (bf16[144,4096]{1,0:T(8,128)(2,1)S(1)}, bf16[144,4096]{1,0:T(8,128)(2,1)}, u32[]{:S(2)}, u32[]{:S(2)}) collective-permute-start(bf16[144,4096]{1,0:T(8,128)(2,1)S(1)} %slice.32), channel_id=1, source_target_pairs={{32,0},{48,16},{64,32},{80,48},{96,64},{112,80},{0,96},{16,112},{3... | collective-permute-start | bytes 3538952 | tf_op jit(solution)/shard_map/ppermute | solution.py:52
  80.5 25.2 %collective-permute-start.24 = (bf16[128,4096]{1,0:T(8,128)(2,1)S(1)}, bf16[128,4096]{1,0:T(8,128)(2,1)S(1)}, u32[]{:S(2)}, u32[]{:S(2)}) collective-permute-start(bf16[128,4096]{1,0:T(8,128)(2,1)S(1)} %collective-permute-done.14.refs_1_), channel_id=1, source_target_pairs={{1,0},{2,1},{3,2},{0,3},{5,4},{6,5},{7,6},{4,7},{9,8},{10,9},{11,1... | collective-permute-start | bytes 3145736 | tf_op jit(solution)/shard_map/ppermute | solution.py:47
  84.6 25.9 %collective-permute-start.7 = (bf16[144,4096]{1,0:T(8,128)(2,1)}, bf16[144,4096]{1,0:T(8,128)(2,1)}, u32[]{:S(2)}, u32[]{:S(2)}) collective-permute-start(bf16[144,4096]{1,0:T(8,128)(2,1)} %slice.33), channel_id=1, source_target_pairs={{96,0},{112,16},{0,32},{16,48},{32,64},{48,80},{64,96},{80,112},{9... | collective-permute-start | bytes 3538952 | tf_op jit(solution)/shard_map/ppermute | solution.py:52
  85.0 49.0 %collective-permute-start.10 = (bf16[288,4096]{1,0:T(8,128)(2,1)}, bf16[288,4096]{1,0:T(8,128)(2,1)}, u32[]{:S(2)}, u32[]{:S(2)}) collective-permute-start(bf16[288,4096]{1,0:T(8,128)(2,1)} %collective-permute-done.5.refs_7_.refs_6_), channel_id=1, source_target_pairs={{16,0},{0,16},{48,32},{32,48},{80,64},{64,80},{112,96},{96,112},{1... | collective-permute-start | bytes 7077896 | tf_op jit(solution)/shard_map/ppermute | solution.py:57
  85.0 52.2 %collective-permute-start.9 = (bf16[288,4096]{1,0:T(8,128)(2,1)S(1)}, bf16[288,4096]{1,0:T(8,128)(2,1)}, u32[]{:S(2)}, u32[]{:S(2)}) collective-permute-start(bf16[288,4096]{1,0:T(8,128)(2,1)S(1)} %collective-permute-done.4.refs_6_.refs_5_), channel_id=1, source_target_pairs={{16,0},{0,16},{48,32},{32,48},{80,64},{64,80},{112,96},{96,112},{1... | collective-permute-start | bytes 7077896 | tf_op jit(solution)/shard_map/ppermute | solution.py:57
  104.8 26.3 %collective-permute-start.11 = (bf16[144,4096]{1,0:T(8,128)(2,1)}, bf16[144,4096]{1,0:T(8,128)(2,1)}, u32[]{:S(2)}, u32[]{:S(2)}) collective-permute-start(bf16[144,4096]{1,0:T(8,128)(2,1)} %collective-permute-done.6.refs_8_.refs_7_), channel_id=1, source_target_pairs={{16,0},{0,16},{48,32},{32,48},{80,64},{64,80},{112,96},{96,112},{1... | collective-permute-start | bytes 3538952 | tf_op jit(solution)/shard_map/ppermute | solution.py:57
  127.9 29.7 %collective-permute-start.20 = (bf16[128,4096]{1,0:T(8,128)(2,1)}, bf16[128,4096]{1,0:T(8,128)(2,1)}, u32[]{:S(2)}, u32[]{:S(2)}) collective-permute-start(bf16[128,4096]{1,0:T(8,128)(2,1)} %copy-done.20), channel_id=1, source_target_pairs={{1,0},{2,1},{3,2},{0,3},{5,4},{6,5},{7,6},{4,7},{9,8},{10,9},{11,1... | collective-permute-start | bytes 3145736 | tf_op jit(solution)/shard_map/ppermute | solution.py:47
  131.1 26.5 %collective-permute-start.19 = (bf16[128,4096]{1,0:T(8,128)(2,1)}, bf16[128,4096]{1,0:T(8,128)(2,1)}, u32[]{:S(2)}, u32[]{:S(2)}) collective-permute-start(bf16[128,4096]{1,0:T(8,128)(2,1)} %collective-permute-done.refs_1_), channel_id=1, source_target_pairs={{4,0},{5,1},{6,2},{7,3},{8,4},{9,5},{10,6},{11,7},{12,8},{13,9},{1... | collective-permute-start | bytes 3145736 | tf_op jit(solution)/shard_map/ppermute | solution.py:47
  133.9 60.5 %collective-permute-start.15 = (bf16[128,4096]{1,0:T(8,128)(2,1)}, bf16[128,4096]{1,0:T(8,128)(2,1)}, u32[]{:S(2)}, u32[]{:S(2)}) collective-permute-start(bf16[128,4096]{1,0:T(8,128)(2,1)} %collective-permute-done.refs_1_), channel_id=1, source_target_pairs={{3,0},{0,1},{1,2},{2,3},{7,4},{4,5},{5,6},{6,7},{11,8},{8,9},{9,10... | collective-permute-start | bytes 3145736 | tf_op jit(solution)/shard_map/ppermute | solution.py:47
  134.0 61.3 %collective-permute-start.16 = (bf16[128,4096]{1,0:T(8,128)(2,1)}, bf16[128,4096]{1,0:T(8,128)(2,1)}, u32[]{:S(2)}, u32[]{:S(2)}) collective-permute-start(bf16[128,4096]{1,0:T(8,128)(2,1)} %copy-done.21), channel_id=1, source_target_pairs={{1,0},{2,1},{3,2},{0,3},{5,4},{6,5},{7,6},{4,7},{9,8},{10,9},{11,1... | collective-permute-start | bytes 3145736 | tf_op jit(solution)/shard_map/ppermute | solution.py:47
  151.2 60.3 %collective-permute-start.25 = (bf16[64,4096]{1,0:T(8,128)(2,1)S(1)}, bf16[64,4096]{1,0:T(8,128)(2,1)S(1)}, u32[]{:S(2)}, u32[]{:S(2)}) collective-permute-start(bf16[64,4096]{1,0:T(8,128)(2,1)S(1)} %get-tuple-element.26), channel_id=1, source_target_pairs={{4,0},{5,1},{6,2},{7,3},{8,4},{9,5},{10,6},{11,7},{12,8},{13,9},{1... | collective-permute-start | bytes 1572872 | tf_op jit(solution)/shard_map/ppermute | solution.py:47
  173.8 38.5 %collective-permute-start.27 = (bf16[64,4096]{1,0:T(8,128)(2,1)S(1)}, bf16[64,4096]{1,0:T(8,128)(2,1)}, u32[]{:S(2)}, u32[]{:S(2)}) collective-permute-start(bf16[64,4096]{1,0:T(8,128)(2,1)S(1)} %get-tuple-element.28), channel_id=1, source_target_pairs={{1,0},{2,1},{3,2},{0,3},{5,4},{6,5},{7,6},{4,7},{9,8},{10,9},{11,1... | collective-permute-start | bytes 1572872 | tf_op jit(solution)/shard_map/ppermute | solution.py:47
  174.9 40.3 %collective-permute-start.32 = (bf16[128,4096]{1,0:T(8,128)(2,1)S(1)}, bf16[128,4096]{1,0:T(8,128)(2,1)}, u32[]{:S(2)}, u32[]{:S(2)}) collective-permute-start(bf16[128,4096]{1,0:T(8,128)(2,1)S(1)} %get-tuple-element.32), channel_id=1, source_target_pairs={{12,0},{13,1},{14,2},{15,3},{0,4},{1,5},{2,6},{3,7},{4,8},{5,9},{6... | collective-permute-start | bytes 3145736 | tf_op jit(solution)/shard_map/ppermute | solution.py:47
  194.4 27.6 %collective-permute-start.33 = (bf16[128,4096]{1,0:T(8,128)(2,1)}, bf16[128,4096]{1,0:T(8,128)(2,1)}, u32[]{:S(2)}, u32[]{:S(2)}) collective-permute-start(bf16[128,4096]{1,0:T(8,128)(2,1)} %get-tuple-element.33), channel_id=1, source_target_pairs={{3,0},{0,1},{1,2},{2,3},{7,4},{4,5},{5,6},{6,7},{11,8},{8,9},{9,10... | collective-permute-start | bytes 3145736 | tf_op jit(solution)/shard_map/ppermute | solution.py:47
  195.3 91.8 %collective-permute-start.31 = (bf16[128,4096]{1,0:T(8,128)(2,1)}, bf16[128,4096]{1,0:T(8,128)(2,1)S(1)}, u32[]{:S(2)}, u32[]{:S(2)}) collective-permute-start(bf16[128,4096]{1,0:T(8,128)(2,1)} %get-tuple-element.30), channel_id=1, source_target_pairs={{3,0},{0,1},{1,2},{2,3},{7,4},{4,5},{5,6},{6,7},{11,8},{8,9},{9,10... | collective-permute-start | bytes 3145736 | tf_op jit(solution)/shard_map/ppermute | solution.py:47
  211.6 51.8 %collective-permute-start.36 = (bf16[128,4096]{1,0:T(8,128)(2,1)}, bf16[128,4096]{1,0:T(8,128)(2,1)S(1)}, u32[]{:S(2)}, u32[]{:S(2)}) collective-permute-start(bf16[128,4096]{1,0:T(8,128)(2,1)} %get-tuple-element.35), channel_id=1, source_target_pairs={{3,0},{0,1},{1,2},{2,3},{7,4},{4,5},{5,6},{6,7},{11,8},{8,9},{9,10... | collective-permute-start | bytes 3145736 | tf_op jit(solution)/shard_map/ppermute | solution.py:47
  212.3 55.1 %collective-permute-start.38 = (bf16[128,4096]{1,0:T(8,128)(2,1)S(1)}, bf16[128,4096]{1,0:T(8,128)(2,1)S(1)}, u32[]{:S(2)}, u32[]{:S(2)}) collective-permute-start(bf16[128,4096]{1,0:T(8,128)(2,1)S(1)} %get-tuple-element.37), channel_id=1, source_target_pairs={{12,0},{13,1},{14,2},{15,3},{0,4},{1,5},{2,6},{3,7},{4,8},{5,9},{6... | collective-permute-start | bytes 3145736 | tf_op jit(solution)/shard_map/ppermute | solution.py:47
  215.2 48.5 %collective-permute-start.26 = (bf16[128,4096]{1,0:T(8,128)(2,1)S(1)}, bf16[128,4096]{1,0:T(8,128)(2,1)S(1)}, u32[]{:S(2)}, u32[]{:S(2)}) collective-permute-start(bf16[128,4096]{1,0:T(8,128)(2,1)S(1)} %pad_maximum_fusion.1), channel_id=1, source_target_pairs={{1,0},{2,1},{3,2},{0,3},{5,4},{6,5},{7,6},{4,7},{9,8},{10,9},{11,1... | collective-permute-start | bytes 3145736 | tf_op jit(solution)/shard_map/ppermute | solution.py:47
  222.0 43.2 %collective-permute-start.28 = (bf16[128,4096]{1,0:T(8,128)(2,1)S(1)}, bf16[128,4096]{1,0:T(8,128)(2,1)S(1)}, u32[]{:S(2)}, u32[]{:S(2)}) collective-permute-start(bf16[128,4096]{1,0:T(8,128)(2,1)S(1)} %pad_maximum_fusion.2), channel_id=1, source_target_pairs={{4,0},{5,1},{6,2},{7,3},{8,4},{9,5},{10,6},{11,7},{12,8},{13,9},{1... | collective-permute-start | bytes 3145736 | tf_op jit(solution)/shard_map/ppermute | solution.py:47
  265.2 44.2 %collective-permute-start.37 = (bf16[128,4096]{1,0:T(8,128)(2,1)S(1)}, bf16[128,4096]{1,0:T(8,128)(2,1)S(1)}, u32[]{:S(2)}, u32[]{:S(2)}) collective-permute-start(bf16[128,4096]{1,0:T(8,128)(2,1)S(1)} %add_convert_fusion.2), channel_id=1, source_target_pairs={{4,0},{5,1},{6,2},{7,3},{8,4},{9,5},{10,6},{11,7},{12,8},{13,9},{1... | collective-permute-start | bytes 3145736 | tf_op jit(solution)/shard_map/ppermute | solution.py:47
  267.5 41.6 %collective-permute-start.29 = (bf16[128,4096]{1,0:T(8,128)(2,1)S(1)}, bf16[128,4096]{1,0:T(8,128)(2,1)S(1)}, u32[]{:S(2)}, u32[]{:S(2)}) collective-permute-start(bf16[128,4096]{1,0:T(8,128)(2,1)S(1)} %add_convert_fusion.6), channel_id=1, source_target_pairs={{4,0},{5,1},{6,2},{7,3},{8,4},{9,5},{10,6},{11,7},{12,8},{13,9},{1... | collective-permute-start | bytes 3145736 | tf_op jit(solution)/shard_map/ppermute | solution.py:47
  (34 other events, 1359.8 us)
where the time goes:
time: 333 us; the launch traced here: 332 us
  waiting for transfers between devices  193 us (58%)
  Pallas kernels  64 us (19%)
  starting transfers between devices  57 us (17%)
  other arithmetic  10.1 us (3%)
  local copies, waits for them, and re-layouts  6.86 us (2%)
    ppermute x32, waiting for transfers between devices, get_exp(): return lax.ppermute(x, 'exp', pairs)  156 us
    pallas_call x4, Pallas kernels, expert_blocks(): pl.pallas_call(functools.partial(expert_body, nb, parts, pieces), out_sha...  64 us
    ppermute x32, starting transfers between devices, get_exp(): return lax.ppermute(x, 'exp', pairs)  46.5 us
    ppermute x4, waiting for transfers between devices, get_x(): return lax.ppermute(v, 'grp', pairs)  37.6 us
    convert_element_type x9, other arithmetic, add_up(): pieces.append(total.astype(jnp.bfloat16))  7.02 us
  transfers between devices with their start and end apart: 42, of which 16 were waited for; matrix products, arithmetic and copies ran while one was open for 4% of the time, Pallas kernels for 19%

commit v1 on v0

--- a/solution.py
+++ b/solution.py
@@ -19,12 +19,12 @@
     (-1, 0): [(0, 128, (-1, 0), (0, 0))],
     (0, 1): [(0, 128, (0, 1), (0, 0))],
     (0, -1): [(0, 128, (0, -1), (0, 0))],
-    (-1, -1): [(0, 128, (-1, 0), (0, -1))],
+    (-1, -1): [(0, 64, (-1, 0), (0, -1)), (64, 64, (-1, 0), (0, -1))],
     (1, -1): [(0, 128, (0, -1), (1, 0))],
     (-1, 1): [(0, 128, (0, 1), (-1, 0))],
     (1, 1): [(0, 128, (1, 0), (0, 1))],
-    (2, -1): [(0, 128, (-1, 0), (-1, -1))],
-    (-1, 2): [(0, 128, (0, -1), (-1, -1))],
+    (2, -1): [(0, 64, (-1, 0), (-1, -1)), (64, 64, (-1, 0), (-1, -1))],
+    (-1, 2): [(0, 64, (0, -1), (-1, -1)), (64, 64, (0, -1), (-1, -1))],
     (0, 2): [(0, 128, (0, 1), (0, 1))],
     (2, 0): [(0, 128, (1, 0), (1, 0))],
     (2, 2): [(0, 64, (0, -1), (2, -1)), (64, 64, (-1, 0), (-1, 2))],
@@ -32,11 +32,20 @@
     (2, 1): [(0, 128, (1, 0), (1, 1))],
 }
 
+WHOLE = {o: [(0, 128) + parts[0][2:]] for o, parts in TREE.items()}
+BACK = {
+    **WHOLE,
+    (2, 2): TREE[2, 2],
+    (2, 0): [(0, 96, (1, 0), (1, 0)), (96, 32, (-1, 0), (-1, 0))],
+    (0, 2): [(0, 96, (0, 1), (0, 1)), (96, 32, (0, -1), (0, -1))],
+}
+
 BATCHES = [
     [(2, 2), (2, 1), (1, 2)],
     [(2, -1), (-1, 2), (2, 0), (0, 2)],
     [(-1, -1), (1, 1), (1, -1), (-1, 1)],
-    [(0, 0), (1, 0), (-1, 0), (0, 1), (0, -1)],
+    [(1, 0), (-1, 0), (0, 1), (0, -1)],
+    [(0, 0)],
 ]
 
 
@@ -57,17 +66,34 @@
     return lax.ppermute(v, "grp", pairs)
 
 
-def gather_weights(w):
-    half = w.shape[0] // 2
-    right = get_x(w, 1)
-    left = get_x(w, -1)
-    far_a = get_x(right[:half], 1)
-    far_b = get_x(left[half:], -1)
-    mine = [w, right, left, far_a, far_b]
+def gather_weights(gate, up, down):
+    mid = gate.shape[0] // 2
+    own = [
+        jnp.concatenate([gate, up[:mid]], axis=0),
+        jnp.concatenate([up[mid:], down], axis=0),
+    ]
+    right, left = [None, None], [None, None]
+    for i in (0, 1):
+        right[i] = get_x(own[i], 1)
+        left[i] = get_x(own[i], -1)
+    far = []
+    for i, near in enumerate((right[0], left[1])):
+        far.append(get_x(near, 1 - 2 * i))
+    mine = own + right + left + far
     other = []
     for v in mine:
         other.append(get_core(v))
     return mine + other
+
+
+def take(parts, row, rows):
+    at = 0
+    for part in parts:
+        size = part.shape[0]
+        if at <= row and row + rows <= at + size:
+            return part if size == rows else part[row - at : row - at + rows]
+        at += size
+    raise ValueError("part")
 
 
 def gather_tokens(t):
@@ -75,29 +101,25 @@
     for offset, parts in TREE.items():
         blocks[offset] = []
         for row, rows, way, before in parts:
-            (source,) = blocks[before]
-            if rows < source.shape[0]:
-                source = source[row : row + rows]
+            source = take(blocks[before], row, rows)
             blocks[offset].append(get_exp(source, *way))
     return blocks
 
 
 def add_up(value, extra):
     rows = value.shape[0]
-    cuts = sorted({0, rows} | {r for r, _ in extra} | {r + v.shape[0] for r, v in extra})
-    pieces = []
-    for lo, hi in zip(cuts, cuts[1:]):
-        total = value[lo:hi].astype(jnp.float32)
-        for row, v in extra:
-            if row <= lo and hi <= row + v.shape[0]:
-                total = total + v[lo - row : hi - row].astype(jnp.float32)
-        pieces.append(total.astype(jnp.bfloat16))
-    return pieces[0] if len(pieces) == 1 else jnp.concatenate(pieces, axis=0)
+    total = value.astype(jnp.float32)
+    for row, v in extra:
+        below = rows - row - v.shape[0]
+        if row or below:
+            v = jnp.pad(v, ((row, below), (0, 0)))
+        total = total + v.astype(jnp.float32)
+    return total.astype(jnp.bfloat16)
 
 
 def reduce_back(partial):
     extra = {offset: [] for offset in partial}
-    for offset, parts in reversed(TREE.items()):
+    for offset, parts in reversed(BACK.items()):
         values = partial[offset]
         if extra[offset]:
             values = [add_up(values[0], extra[offset])]
@@ -116,25 +138,23 @@
             pieces.append((operand, row, kind, to, part))
             row, to, count = row + part, to + part, count - part
 
-    for core in range(2):
-        for k in range(3):
-            for kind in range(3):
-                cut(core * 5 + k, kind * n, kind, (core * 4 + k) * n, n)
+    for shard in range(8):
         for kind in range(3):
             lo, hi = kind * n, (kind + 1) * n
-            base = (core * 4 + 3) * n
-            for operand, start in ((3, 0), (4, half)):
+            for part in range(2):
+                start = part * half
                 a, b = max(lo, start), min(hi, start + half)
                 if a < b:
-                    cut(core * 5 + operand, a - start, kind, base + a - lo, b - a)
+                    cut(2 * shard + part, a - start, kind, shard * n + a - lo, b - a)
     pieces.sort(key=lambda p: (p[2] == 2, p[3]))
     return pieces
 
 
-def expert_body(nb, parts, pieces, src_ref, meta_ref, *refs):
-    np_ = len(parts)
-    inputs, weights, outs = refs[:np_], refs[np_ : np_ + 10], refs[np_ + 10 : 2 * np_ + 10]
-    w_ref, t_ref, x_ref, h_ref, o_ref, p_ref, s_ref, k_ref, t_sem, w_sem, o_sem = refs[2 * np_ + 10 :]
+def expert_body(nb, parts, out_parts, pieces, src_ref, meta_ref, *refs):
+    weights, refs = refs[:16], refs[16:]
+    inputs, refs = refs[: len(parts)], refs[len(parts) :]
+    outs, refs = refs[: len(out_parts)], refs[len(out_parts) :]
+    w_ref, t_ref, x_ref, h_ref, o_ref, p_ref, s_ref, k_ref, t_sem, w_sem, o_sem = refs
     hidden = w_ref.shape[1]
     width = w_ref.shape[2]
     tiles = hidden // NTILE
@@ -154,7 +174,7 @@
     fetch(0)
 
     def out_copy(i):
-        b, row, rows = parts[i]
+        b, row, rows = out_parts[i]
         return pltpu.make_async_copy(p_ref.at[b, pl.ds(row, rows)], outs[i], o_sem.at[i])
 
     slots = lax.broadcasted_iota(jnp.int32, (CAP, 128), 0).astype(jnp.float32) + 1.0
@@ -199,18 +219,23 @@
         out = jnp.dot(h_ref[...], w_ref[2, :, cols], preferred_element_type=jnp.float32)
         o_ref[:, cols] = (out * jnp.tile(k_ref[...], (1, CTILE // 128))).astype(jnp.bfloat16)
 
-    for b in range(nb):
+    @pl.loop(0, nb)
+    def _(b):
+        rows = pl.ds(pl.multiple_of(b * CAP, CAP), CAP)
         p_ref[b] = jnp.dot(
-            s_ref[b], o_ref[b * CAP : (b + 1) * CAP, :], preferred_element_type=jnp.float32
+            s_ref[b], o_ref[rows, :], preferred_element_type=jnp.float32
         ).astype(jnp.bfloat16)
-        for i, (block, row, rows) in enumerate(parts):
-            if block == b:
+        for i, part in enumerate(out_parts):
+
+            @pl.when(b == part[0])
+            def _():
                 out_copy(i).start()
-    for i in range(np_):
+
+    for i in range(len(out_parts)):
         out_copy(i).wait()
 
 
-def expert_blocks(src, meta, blocks, weights):
+def expert_blocks(src, meta, blocks, weights, cuts):
     nb = len(blocks)
     parts, inputs = [], []
     for b, block in enumerate(blocks):
@@ -220,7 +245,8 @@
             inputs.append(part)
             row += part.shape[0]
     rows, width = row, inputs[0].shape[1]
-    n = weights[0].shape[0] // 3
+    out_parts = [(b, row, size) for b, cut in enumerate(cuts) for row, size in cut]
+    n = 2 * weights[0].shape[0] // 3
     hidden = 8 * n
     pieces = weight_pieces(n)
     m = nb * CAP
@@ -228,14 +254,14 @@
     flops = 2 * m * width * hidden * 3 + 4 * m * rows * width
     moved = 2 * (3 * hidden * width + 2 * nb * rows * width)
     outs = pl.pallas_call(
-        functools.partial(expert_body, nb, parts, pieces),
-        out_shape=[jax.ShapeDtypeStruct(v.shape, jnp.bfloat16) for v in inputs],
+        functools.partial(expert_body, nb, parts, out_parts, pieces),
+        out_shape=[jax.ShapeDtypeStruct((part[2], width), jnp.bfloat16) for part in out_parts],
         in_specs=[
             pl.BlockSpec(memory_space=pltpu.SMEM),
             pl.BlockSpec(memory_space=pltpu.VMEM),
         ]
-        + [anywhere] * (len(parts) + 10),
-        out_specs=[anywhere] * len(parts),
+        + [anywhere] * (16 + len(parts)),
+        out_specs=[anywhere] * len(out_parts),
         scratch_shapes=[
             pltpu.VMEM((3, hidden, width), jnp.bfloat16),
             pltpu.VMEM((nb, rows, width), jnp.bfloat16),
@@ -247,18 +273,18 @@
             pltpu.VMEM((m, 128), jnp.float32),
             pltpu.SemaphoreType.DMA((nb,)),
             pltpu.SemaphoreType.DMA((hidden // NTILE + 1,)),
-            pltpu.SemaphoreType.DMA((len(parts),)),
+            pltpu.SemaphoreType.DMA((len(out_parts),)),
         ],
         compiler_params=pltpu.CompilerParams(vmem_limit_bytes=50 << 20),
         cost_estimate=pl.CostEstimate(flops=flops, bytes_accessed=moved, transcendentals=m * hidden),
-    )(src, meta, *inputs, *weights)
-    return [[v for v, part in zip(outs, parts) if part[0] == b] for b in range(nb)]
+    )(src, meta, *weights, *inputs)
+    return [[v for v, part in zip(outs, out_parts) if part[0] == b] for b in range(nb)]
 
 
 def per_device(tokens, expert_ids, gate_fixed, w_gate, w_up, w_down):
     me = lax.axis_index("exp")
     blocks = gather_tokens(tokens)
-    weights = gather_weights(jnp.concatenate([w_gate[0].T, w_up[0].T, w_down[0]], axis=0))
+    weights = gather_weights(w_gate[0].T, w_up[0].T, w_down[0])
 
     hit = expert_ids.T[None] == jnp.arange(EXPERTS, dtype=jnp.int32)[:, None, None]
     routed = jnp.any(hit, axis=1).astype(jnp.int32)
@@ -272,7 +298,8 @@
         dz = jnp.array([o[0] for o in batch], jnp.int32)
         dy = jnp.array([o[1] for o in batch], jnp.int32)
         src = (((me >> 2) + dz) & 3) * 4 + ((me + dy) & 3)
-        outs = expert_blocks(src, meta, [blocks[o] for o in batch], weights)
+        cuts = [[part[:2] for part in BACK.get(o, [(0, 128)])] for o in batch]
+        outs = expert_blocks(src, meta, [blocks[o] for o in batch], weights, cuts)
         partial.update(zip(batch, outs))
     return reduce_back(partial)
 

time: 333 us -> 317 us (0.952)
  waiting for transfers between devices: 193 us -> 161 us
  starting transfers between devices: 57 us -> 68.3 us
  Pallas kernels: 64 us -> 70.1 us
  local copies, waits for them, and re-layouts: 6.86 us -> 2.06 us
  other arithmetic: 10.1 us -> 13.6 us
    ppermute x32 -> x37, waiting for transfers between devices: 156 us -> 113 us  [get_exp(): return lax.ppermute(x, 'exp', pairs)]
    ppermute x32 -> x37, starting transfers between devices: 46.5 us -> 57.2 us  [get_exp(): return lax.ppermute(x, 'exp', pairs)]
    ppermute x4 -> x6, waiting for transfers between devices: 37.6 us -> 47.7 us  [get_x(): return lax.ppermute(v, 'grp', pairs)]
    pallas_call x4 -> x5, Pallas kernels: 64 us -> 70.1 us  [expert_blocks(): pl.pallas_call(functools.partial(expert_body, nb, parts, out_parts, piece...]
    convert_element_type x9, other arithmetic: 7.02 us -> 12.4 us  [add_up(): return total.astype(jnp.bfloat16)]
    slice x6 -> x2, local copies, waits for them, and re-layouts: 5.26 us -> 1.25 us  [the longest x1 1.17 us: gather_weights(): up[mid:]]
    ppermute x4 -> x6, starting transfers between devices: 4.19 us -> 7.08 us  [get_x(): return lax.ppermute(v, 'grp', pairs)]
  transfers between devices with their start and end apart: 42 -> 52, of which waited for: 16 -> 24; matrix products, arithmetic and copies ran while one was open for 4% -> 3% of each run, Pallas kernels for 19% -> 22%
where the time goes in v1:
time: 317 us; the launch traced here: 315 us
  waiting for transfers between devices  161 us (51%)
  Pallas kernels  70.1 us (22%)
  starting transfers between devices  68.3 us (22%)
  other arithmetic  13.6 us (4%)
    ppermute x37, waiting for transfers between devices, get_exp(): return lax.ppermute(x, 'exp', pairs)  113 us
    pallas_call x5, Pallas kernels, expert_blocks(): pl.pallas_call(functools.partial(expert_body, nb, parts, out_parts, piece...  70.1 us
    ppermute x37, starting transfers between devices, get_exp(): return lax.ppermute(x, 'exp', pairs)  57.2 us
    ppermute x6, waiting for transfers between devices, get_x(): return lax.ppermute(v, 'grp', pairs)  47.7 us
    convert_element_type x9, other arithmetic, add_up(): return total.astype(jnp.bfloat16)  12.4 us
    ppermute x6, starting transfers between devices, get_x(): return lax.ppermute(v, 'grp', pairs)  7.08 us
  transfers between devices with their start and end apart: 52, of which 24 were waited for; matrix products, arithmetic and copies ran while one was open for 3% of the time, Pallas kernels for 22%

profile of v1, /device:TPU:2, one launch (start us, length us, event | category | flops | bytes accessed | tf_op | source)
XLA Modules:
  0.0 315.4 jit_solution(16735353196198863533)
XLA Ops:
  3.2 4.0 %collective-permute-start.14 = (bf16[128,4096]{1,0:T(8,128)(2,1)}, bf16[128,4096]{1,0:T(8,128)(2,1)}, u32[]{:S(2)}, u32[]{:S(2)}) collective-permute-start(bf16[128,4096]{1,0:T(8,128)(2,1)} %refs_16_.1), channel_id=1, source_target_pairs={{4,0},{5,1},{6,2},{7,3},{8,4},{9,5},{10,6},{11,7},{12,8},{13,9},{1... | collective-permute-start | bytes 3145736 | tf_op jit(solution)/shard_map/ppermute | solution.py:56
  10.1 16.3 %collective-permute-done.17.refs_19_ = bf16[128,4096]{1,0:T(8,128)(2,1)S(1)} collective-permute-done((bf16[128,4096]{1,0:T(8,128)(2,1)}, bf16[128,4096]{1,0:T(8,128)(2,1)S(1)}, u32[]{:S(2)}, u32[]{:S(2)}) %collective-permute-start.17) | collective-permute-done | bytes 1048608 | tf_op jit(solution)/shard_map/ppermute | solution.py:56
  32.9 4.7 %collective-permute-done.refs_2_ = bf16[144,4096]{1,0:T(8,128)(2,1)} collective-permute-done((bf16[144,4096]{1,0:T(8,128)(2,1)S(1)}, bf16[144,4096]{1,0:T(8,128)(2,1)}, u32[]{:S(2)}, u32[]{:S(2)}) %collective-permute-start) | collective-permute-done | bytes 1179680 | tf_op jit(solution)/shard_map/ppermute | solution.py:61
  37.6 23.4 %collective-permute-done.1.refs_3_ = bf16[144,4096]{1,0:T(8,128)(2,1)} collective-permute-done((bf16[144,4096]{1,0:T(8,128)(2,1)S(1)}, bf16[144,4096]{1,0:T(8,128)(2,1)}, u32[]{:S(2)}, u32[]{:S(2)}) %collective-permute-start.1) | collective-permute-done | bytes 1179680 | tf_op jit(solution)/shard_map/ppermute | solution.py:61
  61.0 3.0 collective-permute-start.27
  64.3 15.7 %collective-permute-done.3.refs_5_ = bf16[144,4096]{1,0:T(8,128)(2,1)} collective-permute-done((bf16[144,4096]{1,0:T(8,128)(2,1)S(1)}, bf16[144,4096]{1,0:T(8,128)(2,1)}, u32[]{:S(2)}, u32[]{:S(2)}) %collective-permute-start.3) | collective-permute-done | bytes 1179680 | tf_op jit(solution)/shard_map/ppermute | solution.py:61
  85.6 13.0 %collective-permute-done.18.refs_16_ = bf16[64,4096]{1,0:T(8,128)(2,1)S(1)} collective-permute-done((bf16[64,4096]{1,0:T(8,128)(2,1)S(1)}, bf16[64,4096]{1,0:T(8,128)(2,1)S(1)}, u32[]{:S(2)}, u32[]{:S(2)}) %collective-permute-start.18) | collective-permute-done | bytes 524320 | tf_op jit(solution)/shard_map/ppermute | solution.py:56
  98.6 11.2 %collective-permute-done.20.refs_17_ = bf16[64,4096]{1,0:T(8,128)(2,1)S(1)} collective-permute-done((bf16[64,4096]{1,0:T(8,128)(2,1)S(1)}, bf16[64,4096]{1,0:T(8,128)(2,1)S(1)}, u32[]{:S(2)}, u32[]{:S(2)}) %collective-permute-start.20) | collective-permute-done | bytes 524320 | tf_op jit(solution)/shard_map/ppermute | solution.py:56
  109.8 3.0 collective-permute-start.4
  113.0 6.2 %collective-permute-done.19.refs_16_ = bf16[64,4096]{1,0:T(8,128)(2,1)S(1)} collective-permute-done((bf16[64,4096]{1,0:T(8,128)(2,1)S(1)}, bf16[64,4096]{1,0:T(8,128)(2,1)S(1)}, u32[]{:S(2)}, u32[]{:S(2)}) %collective-permute-start.19) | collective-permute-done | bytes 524320 | tf_op jit(solution)/shard_map/ppermute | solution.py:56
  119.9 9.5 %collective-permute-done.21.refs_17_ = bf16[64,4096]{1,0:T(8,128)(2,1)S(1)} collective-permute-done((bf16[64,4096]{1,0:T(8,128)(2,1)S(1)}, bf16[64,4096]{1,0:T(8,128)(2,1)S(1)}, u32[]{:S(2)}, u32[]{:S(2)}) %collective-permute-start.21) | collective-permute-done | bytes 524320 | tf_op jit(solution)/shard_map/ppermute | solution.py:56
  135.9 3.5 %all-to-all-start = ((f32[16,2,128]{2,1,0:T(2,128)}), f32[16,2,128]{2,1,0:T(2,128)S(1)}, u32[]{:S(2)}, u32[]{:S(2)}) async-start(f32[16,2,128]{2,1,0:T(2,128)} %pad_maximum_fusion.2), calls=%async_computation | async-start | bytes 32768 | tf_op jit(solution)/shard_map/all_to_all | solution.py:294
  139.5 3.2 collective-permute-start.24
  146.4 3.1 collective-permute-start.33
  149.5 15.5 %shard_map.157 = (bf16[128,4096]{1,0:T(8,128)(2,1)S(1)}, bf16[128,4096]{1,0:T(8,128)(2,1)S(1)}, bf16[128,4096]{1,0:T(8,128)(2,1)}, bf16[128,4096]{1,0:T(8,128)(2,1)}) custom-call(s32[4]{0:T(128)S(1)} %and_add_fusion.1.src_ref, f32[16,2,128]{2,1,0:T(2,128)S(1)} %all-to-all-done.meta_ref, bf16[144,4096]{1,0:T(8,128)(2,1)} %copy-done, ...), custom_call_target="tpu_custom_call" | custom-call | flops 6710886400 | bytes 27262976 | tf_op jit(solution)/shard_map/pallas_call | solution.py:256
  169.2 3.7 %collective-permute-start.49 = (bf16[128,4096]{1,0:T(8,128)(2,1)}, bf16[128,4096]{1,0:T(8,128)(2,1)}, u32[]{:S(2)}, u32[]{:S(2)}) collective-permute-start(bf16[128,4096]{1,0:T(8,128)(2,1)} %get-tuple-element.40), channel_id=1, source_target_pairs={{1,0},{2,1},{3,2},{0,3},{5,4},{6,5},{7,6},{4,7},{9,8},{10,9},{11,1... | collective-permute-start | bytes 3145736 | tf_op jit(solution)/shard_map/ppermute | solution.py:56
  172.9 15.3 %shard_map.156 = (bf16[128,4096]{1,0:T(8,128)(2,1)}, bf16[128,4096]{1,0:T(8,128)(2,1)}, bf16[96,4096]{1,0:T(8,128)(2,1)S(1)}, bf16[32,4096]{1,0:T(8,128)(2,1)S(1...) custom-call(s32[4]{0:T(128)S(1)} %and_add_fusion.2.src_ref, f32[16,2,128]{2,1,0:T(2,128)S(1)} %all-to-all-done.meta_ref, ...), custom_call_target="tpu_custom_call" | custom-call | flops 6710886400 | bytes 27262976 | tf_op jit(solution)/shard_map/pallas_call | solution.py:256
  188.3 3.4 %collective-permute-done.33.refs_19_ = bf16[128,4096]{1,0:T(8,128)(2,1)} collective-permute-done((bf16[128,4096]{1,0:T(8,128)(2,1)}, bf16[128,4096]{1,0:T(8,128)(2,1)}, u32[]{:S(2)}, u32[]{:S(2)}) %collective-permute-start.33) | collective-permute-done | bytes 1048608 | tf_op jit(solution)/shard_map/ppermute | solution.py:56
  191.6 14.1 %shard_map.158 = (bf16[64,4096]{1,0:T(8,128)(2,1)S(1)}, bf16[64,4096]{1,0:T(8,128)(2,1)S(1)}, bf16[128,4096]{1,0:T(8,128)(2,1)S(1)}, bf16[128,4096]{1,0:T(8,128)(2,1)}) custom-call(s32[3]{0:T(128)S(1)} %and_add_fusion.src_ref, f32[16,2,128]{2,1,0:T(2,128)S(1)} %all-to-all-done.meta_ref, bf16[144,4096]{1,0:T(8,128)(2,1)} %copy-done, ...), custom_call_target="tpu_custom_call" | custom-call | flops 5033164800 | bytes 25165824 | tf_op jit(solution)/shard_map/pallas_call | solution.py:256
  209.7 15.9 %shard_map.155 = (bf16[128,4096]{1,0:T(8,128)(2,1)S(1)}, bf16[128,4096]{1,0:T(8,128)(2,1)S(1)}, bf16[128,4096]{1,0:T(8,128)(2,1)S(1)}, bf16[128,4096]{1,0:T(8,128)(2,1)}) custom-call(s32[4]{0:T(128)S(1)} %and_add_fusion.3.src_ref, f32[16,2,128]{2,1,0:T(2,128)S(1)} %all-to-all-done.meta_ref, bf16[144,4096]{1,0:T(8,128)(2,1)} %copy-done, ...), custom_call_target="tpu_custom_call" | custom-call | flops 6710886400 | bytes 27262976 | tf_op jit(solution)/shard_map/pallas_call | solution.py:256
  225.6 3.4 %collective-permute-start.34 = (bf16[64,4096]{1,0:T(8,128)(2,1)S(1)}, bf16[64,4096]{1,0:T(8,128)(2,1)S(1)}, u32[]{:S(2)}, u32[]{:S(2)}) collective-permute-start(bf16[64,4096]{1,0:T(8,128)(2,1)S(1)} %get-tuple-element.27), channel_id=1, source_target_pairs={{4,0},{5,1},{6,2},{7,3},{8,4},{9,5},{10,6},{11,7},{12,8},{13,9},{1... | collective-permute-start | bytes 1572872 | tf_op jit(solution)/shard_map/ppermute | solution.py:56
  229.2 8.0 %collective-permute-done.34 = bf16[64,4096]{1,0:T(8,128)(2,1)S(1)} collective-permute-done((bf16[64,4096]{1,0:T(8,128)(2,1)S(1)}, bf16[64,4096]{1,0:T(8,128)(2,1)S(1)}, u32[]{:S(2)}, u32[]{:S(2)}) %collective-permute-start.34) | collective-permute-done | bytes 524320 | tf_op jit(solution)/shard_map/ppermute | solution.py:56
  237.6 3.5 %collective-permute-start.37 = (bf16[128,4096]{1,0:T(8,128)(2,1)S(1)}, bf16[128,4096]{1,0:T(8,128)(2,1)S(1)}, u32[]{:S(2)}, u32[]{:S(2)}) collective-permute-start(bf16[128,4096]{1,0:T(8,128)(2,1)S(1)} %add_convert_fusion.7), channel_id=1, source_target_pairs={{4,0},{5,1},{6,2},{7,3},{8,4},{9,5},{10,6},{11,7},{12,8},{13,9},{1... | collective-permute-start | bytes 3145736 | tf_op jit(solution)/shard_map/ppermute | solution.py:56
  241.1 3.2 %collective-permute-start.35 = (bf16[128,4096]{1,0:T(8,128)(2,1)S(1)}, bf16[128,4096]{1,0:T(8,128)(2,1)S(1)}, u32[]{:S(2)}, u32[]{:S(2)}) collective-permute-start(bf16[128,4096]{1,0:T(8,128)(2,1)S(1)} %add_convert_fusion.8), channel_id=1, source_target_pairs={{1,0},{2,1},{3,2},{0,3},{5,4},{6,5},{7,6},{4,7},{9,8},{10,9},{11,1... | collective-permute-start | bytes 3145736 | tf_op jit(solution)/shard_map/ppermute | solution.py:56
  246.3 2.9 add_convert_fusion.1
  249.2 13.6 %collective-permute-done.37 = bf16[128,4096]{1,0:T(8,128)(2,1)S(1)} collective-permute-done((bf16[128,4096]{1,0:T(8,128)(2,1)S(1)}, bf16[128,4096]{1,0:T(8,128)(2,1)S(1)}, u32[]{:S(2)}, u32[]{:S(2)}) %collective-permute-start.37) | collective-permute-done | bytes 1048608 | tf_op jit(solution)/shard_map/ppermute | solution.py:56
  262.8 2.7 collective-permute-start.26
  270.2 7.5 %collective-permute-done.40 = bf16[96,4096]{1,0:T(8,128)(2,1)S(1)} collective-permute-done((bf16[96,4096]{1,0:T(8,128)(2,1)S(1)}, bf16[96,4096]{1,0:T(8,128)(2,1)S(1)}, u32[]{:S(2)}, u32[]{:S(2)}) %collective-permute-start.40) | collective-permute-done | bytes 786464 | tf_op jit(solution)/shard_map/ppermute | solution.py:56
  279.3 13.5 %collective-permute-done.43 = bf16[128,4096]{1,0:T(8,128)(2,1)S(1)} collective-permute-done((bf16[128,4096]{1,0:T(8,128)(2,1)S(1)}, bf16[128,4096]{1,0:T(8,128)(2,1)S(1)}, u32[]{:S(2)}, u32[]{:S(2)}) %collective-permute-start.43) | collective-permute-done | bytes 1048608 | tf_op jit(solution)/shard_map/ppermute | solution.py:56
  295.7 3.1 collective-permute-start.39
  298.8 9.3 %shard_map.154 = bf16[128,4096]{1,0:T(8,128)(2,1)S(1)} custom-call(s32[1]{0:T(128)} %bitcast.src_ref, f32[16,2,128]{2,1,0:T(2,128)S(1)} %all-to-all-done.meta_ref, bf16[144,4096]{1,0:T(8,128)(2,1)S(1)} %copy-done.1, bf16[144,4096]{1,0:T(8,128)(2,1)} %copy-done.3, bf16[144,4096]{1,0:T(8,128)(2,1)} %collective-permute-done.refs_2_, ...), custom_call_target="tpu_custom_call" | custom-call | flops 1677721600 | bytes 20971520 | tf_op jit(solution)/shard_map/pallas_call | solution.py:256
  311.5 4.0 %add_convert_fusion = bf16[128,4096]{1,0:T(8,128)(2,1)} fusion(bf16[128,4096]{1,0:T(8,128)(2,1)} %collective-permute-done.50, bf16[128,4096]{1,0:T(8,128)(2,1)} %collective-permute-done.47, bf16[128,4096]{1,0:T(8,128)(2,1)} %collective-permute-done.44, bf16[128,4096]{1,0:T(8,128)(2,1)} %collective-permute-done.39, bf16[128,4096]{1,0:T(8,128)(2,1)S(1)} %shard_map.154), kind=kLoop, calls=%fused_computation | loop fusion | flops 5242880 | bytes 6291456 | tf_op jit(solution)/shard_map/convert_element_type | solution.py:117
  (155 shorter events, 52.4 us)
Async XLA Ops:
  0.0 26.4 %collective-permute-start.17 = (bf16[128,4096]{1,0:T(8,128)(2,1)}, bf16[128,4096]{1,0:T(8,128)(2,1)S(1)}, u32[]{:S(2)}, u32[]{:S(2)}) collective-permute-start(bf16[128,4096]{1,0:T(8,128)(2,1)} %refs_16_.1), channel_id=1, source_target_pairs={{3,0},{0,1},{1,2},{2,3},{7,4},{4,5},{5,6},{6,7},{11,8},{8,9},{9,10... | collective-permute-start | bytes 3145736 | tf_op jit(solution)/shard_map/ppermute | solution.py:56
  1.6 25.3 %collective-permute-start.16 = (bf16[128,4096]{1,0:T(8,128)(2,1)}, bf16[128,4096]{1,0:T(8,128)(2,1)}, u32[]{:S(2)}, u32[]{:S(2)}) collective-permute-start(bf16[128,4096]{1,0:T(8,128)(2,1)} %refs_16_.1), channel_id=1, source_target_pairs={{1,0},{2,1},{3,2},{0,3},{5,4},{6,5},{7,6},{4,7},{9,8},{10,9},{11,1... | collective-permute-start | bytes 3145736 | tf_op jit(solution)/shard_map/ppermute | solution.py:56
  3.2 26.3 %collective-permute-start.14 = (bf16[128,4096]{1,0:T(8,128)(2,1)}, bf16[128,4096]{1,0:T(8,128)(2,1)}, u32[]{:S(2)}, u32[]{:S(2)}) collective-permute-start(bf16[128,4096]{1,0:T(8,128)(2,1)} %refs_16_.1), channel_id=1, source_target_pairs={{4,0},{5,1},{6,2},{7,3},{8,4},{9,5},{10,6},{11,7},{12,8},{13,9},{1... | collective-permute-start | bytes 3145736 | tf_op jit(solution)/shard_map/ppermute | solution.py:56
  7.3 25.6 %collective-permute-start.15 = (bf16[128,4096]{1,0:T(8,128)(2,1)}, bf16[128,4096]{1,0:T(8,128)(2,1)S(1)}, u32[]{:S(2)}, u32[]{:S(2)}) collective-permute-start(bf16[128,4096]{1,0:T(8,128)(2,1)} %refs_16_.1), channel_id=1, source_target_pairs={{12,0},{13,1},{14,2},{15,3},{0,4},{1,5},{2,6},{3,7},{4,8},{5,9},{6... | collective-permute-start | bytes 3145736 | tf_op jit(solution)/shard_map/ppermute | solution.py:56
  8.6 29.0 %collective-permute-start = (bf16[144,4096]{1,0:T(8,128)(2,1)S(1)}, bf16[144,4096]{1,0:T(8,128)(2,1)}, u32[]{:S(2)}, u32[]{:S(2)}) collective-permute-start(bf16[144,4096]{1,0:T(8,128)(2,1)S(1)} %pad_maximum_fusion.refs_0_), channel_id=1, source_target_pairs={{32,0},{48,16},{64,32},{80,48},{96,64},{112,80},{0,96},{16,112},{3... | collective-permute-start | bytes 3538952 | tf_op jit(solution)/shard_map/ppermute | solution.py:61
  26.4 34.6 %collective-permute-start.1 = (bf16[144,4096]{1,0:T(8,128)(2,1)S(1)}, bf16[144,4096]{1,0:T(8,128)(2,1)}, u32[]{:S(2)}, u32[]{:S(2)}) collective-permute-start(bf16[144,4096]{1,0:T(8,128)(2,1)S(1)} %pad_maximum_fusion.1.refs_1_), channel_id=1, source_target_pairs={{32,0},{48,16},{64,32},{80,48},{96,64},{112,80},{0,96},{16,112},{3... | collective-permute-start | bytes 3538952 | tf_op jit(solution)/shard_map/ppermute | solution.py:61
  26.9 37.1 %collective-permute-start.2 = (bf16[144,4096]{1,0:T(8,128)(2,1)S(1)}, bf16[144,4096]{1,0:T(8,128)(2,1)}, u32[]{:S(2)}, u32[]{:S(2)}) collective-permute-start(bf16[144,4096]{1,0:T(8,128)(2,1)S(1)} %pad_maximum_fusion.refs_0_), channel_id=1, source_target_pairs={{96,0},{112,16},{0,32},{16,48},{32,64},{48,80},{64,96},{80,112},{9... | collective-permute-start | bytes 3538952 | tf_op jit(solution)/shard_map/ppermute | solution.py:61
  29.6 50.5 %collective-permute-start.3 = (bf16[144,4096]{1,0:T(8,128)(2,1)S(1)}, bf16[144,4096]{1,0:T(8,128)(2,1)}, u32[]{:S(2)}, u32[]{:S(2)}) collective-permute-start(bf16[144,4096]{1,0:T(8,128)(2,1)S(1)} %pad_maximum_fusion.1.refs_1_), channel_id=1, source_target_pairs={{96,0},{112,16},{0,32},{16,48},{32,64},{48,80},{64,96},{80,112},{9... | collective-permute-start | bytes 3538952 | tf_op jit(solution)/shard_map/ppermute | solution.py:61
  32.9 48.9 %collective-permute-start.6 = (bf16[144,4096]{1,0:T(8,128)(2,1)S(1)}, bf16[144,4096]{1,0:T(8,128)(2,1)S(1)}, u32[]{:S(2)}, u32[]{:S(2)}) collective-permute-start(bf16[144,4096]{1,0:T(8,128)(2,1)S(1)} %pad_maximum_fusion.refs_0_), channel_id=1, source_target_pairs={{16,0},{0,16},{48,32},{32,48},{80,64},{64,80},{112,96},{96,112},{1... | collective-permute-start | bytes 3538952 | tf_op jit(solution)/shard_map/ppermute | solution.py:66
  37.6 46.1 %collective-permute-start.7 = (bf16[144,4096]{1,0:T(8,128)(2,1)S(1)}, bf16[144,4096]{1,0:T(8,128)(2,1)S(1)}, u32[]{:S(2)}, u32[]{:S(2)}) collective-permute-start(bf16[144,4096]{1,0:T(8,128)(2,1)S(1)} %pad_maximum_fusion.1.refs_1_), channel_id=1, source_target_pairs={{16,0},{0,16},{48,32},{32,48},{80,64},{64,80},{112,96},{96,112},{1... | collective-permute-start | bytes 3538952 | tf_op jit(solution)/shard_map/ppermute | solution.py:66
  61.0 51.7 %collective-permute-start.27 = (bf16[128,4096]{1,0:T(8,128)(2,1)}, bf16[128,4096]{1,0:T(8,128)(2,1)}, u32[]{:S(2)}, u32[]{:S(2)}) collective-permute-start(bf16[128,4096]{1,0:T(8,128)(2,1)} %collective-permute-done.16.refs_18_), channel_id=1, source_target_pairs={{4,0},{5,1},{6,2},{7,3},{8,4},{9,5},{10,6},{11,7},{12,8},{13,9},{1... | collective-permute-start | bytes 3145736 | tf_op jit(solution)/shard_map/ppermute | solution.py:56
  64.0 48.8 %collective-permute-start.28 = (bf16[128,4096]{1,0:T(8,128)(2,1)}, bf16[128,4096]{1,0:T(8,128)(2,1)S(1)}, u32[]{:S(2)}, u32[]{:S(2)}) collective-permute-start(bf16[128,4096]{1,0:T(8,128)(2,1)} %collective-permute-done.14.refs_16_), channel_id=1, source_target_pairs={{3,0},{0,1},{1,2},{2,3},{7,4},{4,5},{5,6},{6,7},{11,8},{8,9},{9,10... | collective-permute-start | bytes 3145736 | tf_op jit(solution)/shard_map/ppermute | solution.py:56
  80.1 32.8 %collective-permute-start.29 = (bf16[128,4096]{1,0:T(8,128)(2,1)S(1)}, bf16[128,4096]{1,0:T(8,128)(2,1)S(1)}, u32[]{:S(2)}, u32[]{:S(2)}) collective-permute-start(bf16[128,4096]{1,0:T(8,128)(2,1)S(1)} %collective-permute-done.15.refs_17_), channel_id=1, source_target_pairs={{1,0},{2,1},{3,2},{0,3},{5,4},{6,5},{7,6},{4,7},{9,8},{10,9},{11,1... | collective-permute-start | bytes 3145736 | tf_op jit(solution)/shard_map/ppermute | solution.py:56
  83.7 26.1 %collective-permute-start.20 = (bf16[64,4096]{1,0:T(8,128)(2,1)S(1)}, bf16[64,4096]{1,0:T(8,128)(2,1)S(1)}, u32[]{:S(2)}, u32[]{:S(2)}) collective-permute-start(bf16[64,4096]{1,0:T(8,128)(2,1)S(1)} %get-tuple-element.41), channel_id=1, source_target_pairs={{12,0},{13,1},{14,2},{15,3},{0,4},{1,5},{2,6},{3,7},{4,8},{5,9},{6... | collective-permute-start | bytes 1572872 | tf_op jit(solution)/shard_map/ppermute | solution.py:56
  139.5 27.0 %collective-permute-start.24 = (bf16[128,4096]{1,0:T(8,128)(2,1)}, bf16[128,4096]{1,0:T(8,128)(2,1)}, u32[]{:S(2)}, u32[]{:S(2)}) collective-permute-start(bf16[128,4096]{1,0:T(8,128)(2,1)} %collective-permute-done.14.refs_16_), channel_id=1, source_target_pairs={{4,0},{5,1},{6,2},{7,3},{8,4},{9,5},{10,6},{11,7},{12,8},{13,9},{1... | collective-permute-start | bytes 3145736 | tf_op jit(solution)/shard_map/ppermute | solution.py:56
  142.6 26.6 %collective-permute-start.25 = (bf16[128,4096]{1,0:T(8,128)(2,1)}, bf16[128,4096]{1,0:T(8,128)(2,1)}, u32[]{:S(2)}, u32[]{:S(2)}) collective-permute-start(bf16[128,4096]{1,0:T(8,128)(2,1)} %collective-permute-done.16.refs_18_), channel_id=1, source_target_pairs={{1,0},{2,1},{3,2},{0,3},{5,4},{6,5},{7,6},{4,7},{9,8},{10,9},{11,1... | collective-permute-start | bytes 3145736 | tf_op jit(solution)/shard_map/ppermute | solution.py:56
  145.5 42.8 %collective-permute-start.32 = (bf16[128,4096]{1,0:T(8,128)(2,1)}, bf16[128,4096]{1,0:T(8,128)(2,1)}, u32[]{:S(2)}, u32[]{:S(2)}) collective-permute-start(bf16[128,4096]{1,0:T(8,128)(2,1)} %collective-permute-done.27.refs_18_), channel_id=1, source_target_pairs={{4,0},{5,1},{6,2},{7,3},{8,4},{9,5},{10,6},{11,7},{12,8},{13,9},{1... | collective-permute-start | bytes 3145736 | tf_op jit(solution)/shard_map/ppermute | solution.py:56
  146.4 45.3 %collective-permute-start.33 = (bf16[128,4096]{1,0:T(8,128)(2,1)}, bf16[128,4096]{1,0:T(8,128)(2,1)}, u32[]{:S(2)}, u32[]{:S(2)}) collective-permute-start(bf16[128,4096]{1,0:T(8,128)(2,1)} %collective-permute-done.27.refs_18_), channel_id=1, source_target_pairs={{1,0},{2,1},{3,2},{0,3},{5,4},{6,5},{7,6},{4,7},{9,8},{10,9},{11,1... | collective-permute-start | bytes 3145736 | tf_op jit(solution)/shard_map/ppermute | solution.py:56
  165.1 23.1 %collective-permute-start.30 = (bf16[64,4096]{1,0:T(8,128)(2,1)S(1)}, bf16[64,4096]{1,0:T(8,128)(2,1)S(1)}, u32[]{:S(2)}, u32[]{:S(2)}) collective-permute-start(bf16[64,4096]{1,0:T(8,128)(2,1)S(1)} %collective-permute-done.19.refs_16_), channel_id=1, source_target_pairs={{3,0},{0,1},{1,2},{2,3},{7,4},{4,5},{5,6},{6,7},{11,8},{8,9},{9,10... | collective-permute-start | bytes 1572872 | tf_op jit(solution)/shard_map/ppermute | solution.py:56
  169.2 77.1 %collective-permute-start.49 = (bf16[128,4096]{1,0:T(8,128)(2,1)}, bf16[128,4096]{1,0:T(8,128)(2,1)}, u32[]{:S(2)}, u32[]{:S(2)}) collective-permute-start(bf16[128,4096]{1,0:T(8,128)(2,1)} %get-tuple-element.40), channel_id=1, source_target_pairs={{1,0},{2,1},{3,2},{0,3},{5,4},{6,5},{7,6},{4,7},{9,8},{10,9},{11,1... | collective-permute-start | bytes 3145736 | tf_op jit(solution)/shard_map/ppermute | solution.py:56
  188.1 58.0 %collective-permute-start.48 = (bf16[96,4096]{1,0:T(8,128)(2,1)S(1)}, bf16[96,4096]{1,0:T(8,128)(2,1)}, u32[]{:S(2)}, u32[]{:S(2)}) collective-permute-start(bf16[96,4096]{1,0:T(8,128)(2,1)S(1)} %get-tuple-element.39), channel_id=1, source_target_pairs={{12,0},{13,1},{14,2},{15,3},{0,4},{1,5},{2,6},{3,7},{4,8},{5,9},{6... | collective-permute-start | bytes 2359304 | tf_op jit(solution)/shard_map/ppermute | solution.py:56
  205.7 31.9 %collective-permute-start.42 = (bf16[128,4096]{1,0:T(8,128)(2,1)}, bf16[128,4096]{1,0:T(8,128)(2,1)S(1)}, u32[]{:S(2)}, u32[]{:S(2)}) collective-permute-start(bf16[128,4096]{1,0:T(8,128)(2,1)} %get-tuple-element.34), channel_id=1, source_target_pairs={{3,0},{0,1},{1,2},{2,3},{7,4},{4,5},{5,6},{6,7},{11,8},{8,9},{9,10... | collective-permute-start | bytes 3145736 | tf_op jit(solution)/shard_map/ppermute | solution.py:56
  207.1 34.0 %collective-permute-start.41 = (bf16[128,4096]{1,0:T(8,128)(2,1)S(1)}, bf16[128,4096]{1,0:T(8,128)(2,1)}, u32[]{:S(2)}, u32[]{:S(2)}) collective-permute-start(bf16[128,4096]{1,0:T(8,128)(2,1)S(1)} %get-tuple-element.33), channel_id=1, source_target_pairs={{12,0},{13,1},{14,2},{15,3},{0,4},{1,5},{2,6},{3,7},{4,8},{5,9},{6... | collective-permute-start | bytes 3145736 | tf_op jit(solution)/shard_map/ppermute | solution.py:56
  237.2 30.3 %collective-permute-start.46 = (bf16[128,4096]{1,0:T(8,128)(2,1)S(1)}, bf16[128,4096]{1,0:T(8,128)(2,1)S(1)}, u32[]{:S(2)}, u32[]{:S(2)}) collective-permute-start(bf16[128,4096]{1,0:T(8,128)(2,1)S(1)} %copy-done.24), channel_id=1, source_target_pairs={{3,0},{0,1},{1,2},{2,3},{7,4},{4,5},{5,6},{6,7},{11,8},{8,9},{9,10... | collective-permute-start | bytes 3145736 | tf_op jit(solution)/shard_map/ppermute | solution.py:56
  237.6 25.2 %collective-permute-start.37 = (bf16[128,4096]{1,0:T(8,128)(2,1)S(1)}, bf16[128,4096]{1,0:T(8,128)(2,1)S(1)}, u32[]{:S(2)}, u32[]{:S(2)}) collective-permute-start(bf16[128,4096]{1,0:T(8,128)(2,1)S(1)} %add_convert_fusion.7), channel_id=1, source_target_pairs={{4,0},{5,1},{6,2},{7,3},{8,4},{9,5},{10,6},{11,7},{12,8},{13,9},{1... | collective-permute-start | bytes 3145736 | tf_op jit(solution)/shard_map/ppermute | solution.py:56
  241.1 24.4 %collective-permute-start.35 = (bf16[128,4096]{1,0:T(8,128)(2,1)S(1)}, bf16[128,4096]{1,0:T(8,128)(2,1)S(1)}, u32[]{:S(2)}, u32[]{:S(2)}) collective-permute-start(bf16[128,4096]{1,0:T(8,128)(2,1)S(1)} %add_convert_fusion.8), channel_id=1, source_target_pairs={{1,0},{2,1},{3,2},{0,3},{5,4},{6,5},{7,6},{4,7},{9,8},{10,9},{11,1... | collective-permute-start | bytes 3145736 | tf_op jit(solution)/shard_map/ppermute | solution.py:56
  246.3 31.3 %collective-permute-start.40 = (bf16[96,4096]{1,0:T(8,128)(2,1)S(1)}, bf16[96,4096]{1,0:T(8,128)(2,1)S(1)}, u32[]{:S(2)}, u32[]{:S(2)}) collective-permute-start(bf16[96,4096]{1,0:T(8,128)(2,1)S(1)} %copy-done.26), channel_id=1, source_target_pairs={{3,0},{0,1},{1,2},{2,3},{7,4},{4,5},{5,6},{6,7},{11,8},{8,9},{9,10... | collective-permute-start | bytes 2359304 | tf_op jit(solution)/shard_map/ppermute | solution.py:56
  262.8 31.5 %collective-permute-start.26 = (bf16[32,4096]{1,0:T(8,128)(2,1)S(1)}, bf16[32,4096]{1,0:T(8,128)(2,1)S(1)}, u32[]{:S(2)}, u32[]{:S(2)}) collective-permute-start(bf16[32,4096]{1,0:T(8,128)(2,1)S(1)} %get-tuple-element.24), channel_id=1, source_target_pairs={{1,0},{2,1},{3,2},{0,3},{5,4},{6,5},{7,6},{4,7},{9,8},{10,9},{11,1... | collective-permute-start | bytes 786440 | tf_op jit(solution)/shard_map/ppermute | solution.py:56
  265.6 27.2 %collective-permute-start.43 = (bf16[128,4096]{1,0:T(8,128)(2,1)S(1)}, bf16[128,4096]{1,0:T(8,128)(2,1)S(1)}, u32[]{:S(2)}, u32[]{:S(2)}) collective-permute-start(bf16[128,4096]{1,0:T(8,128)(2,1)S(1)} %add_convert_fusion.4), channel_id=1, source_target_pairs={{12,0},{13,1},{14,2},{15,3},{0,4},{1,5},{2,6},{3,7},{4,8},{5,9},{6... | collective-permute-start | bytes 3145736 | tf_op jit(solution)/shard_map/ppermute | solution.py:56
  266.7 41.5 %collective-permute-start.50 = (bf16[128,4096]{1,0:T(8,128)(2,1)}, bf16[128,4096]{1,0:T(8,128)(2,1)}, u32[]{:S(2)}, u32[]{:S(2)}) collective-permute-start(bf16[128,4096]{1,0:T(8,128)(2,1)} %add_convert_fusion.1), channel_id=1, source_target_pairs={{12,0},{13,1},{14,2},{15,3},{0,4},{1,5},{2,6},{3,7},{4,8},{5,9},{6... | collective-permute-start | bytes 3145736 | tf_op jit(solution)/shard_map/ppermute | solution.py:56
  267.5 27.0 %collective-permute-start.38 = (bf16[128,4096]{1,0:T(8,128)(2,1)S(1)}, bf16[128,4096]{1,0:T(8,128)(2,1)S(1)}, u32[]{:S(2)}, u32[]{:S(2)}) collective-permute-start(bf16[128,4096]{1,0:T(8,128)(2,1)S(1)} %add_convert_fusion.6), channel_id=1, source_target_pairs={{4,0},{5,1},{6,2},{7,3},{8,4},{9,5},{10,6},{11,7},{12,8},{13,9},{1... | collective-permute-start | bytes 3145736 | tf_op jit(solution)/shard_map/ppermute | solution.py:56
  277.6 33.1 %collective-permute-start.47 = (bf16[128,4096]{1,0:T(8,128)(2,1)S(1)}, bf16[128,4096]{1,0:T(8,128)(2,1)}, u32[]{:S(2)}, u32[]{:S(2)}) collective-permute-start(bf16[128,4096]{1,0:T(8,128)(2,1)S(1)} %add_convert_fusion.2), channel_id=1, source_target_pairs={{4,0},{5,1},{6,2},{7,3},{8,4},{9,5},{10,6},{11,7},{12,8},{13,9},{1... | collective-permute-start | bytes 3145736 | tf_op jit(solution)/shard_map/ppermute | solution.py:56
  (47 other events, 2144.4 us)

commit v2 on v1

--- a/solution.py
+++ b/solution.py
@@ -11,7 +11,7 @@
 EXPERTS = 16
 CAP = 80
 NTILE = 256
-CTILE = 512
+CTILE = 1024
 
 
 TREE = {
@@ -32,20 +32,14 @@
     (2, 1): [(0, 128, (1, 0), (1, 1))],
 }
 
-WHOLE = {o: [(0, 128) + parts[0][2:]] for o, parts in TREE.items()}
-BACK = {
-    **WHOLE,
-    (2, 2): TREE[2, 2],
-    (2, 0): [(0, 96, (1, 0), (1, 0)), (96, 32, (-1, 0), (-1, 0))],
-    (0, 2): [(0, 96, (0, 1), (0, 1)), (96, 32, (0, -1), (0, -1))],
-}
+BACK = {o: [(0, 128) + parts[0][2:]] for o, parts in TREE.items()}
+BACK[2, 2] = TREE[2, 2]
 
 BATCHES = [
     [(2, 2), (2, 1), (1, 2)],
     [(2, -1), (-1, 2), (2, 0), (0, 2)],
     [(-1, -1), (1, 1), (1, -1), (-1, 1)],
-    [(1, 0), (-1, 0), (0, 1), (0, -1)],
-    [(0, 0)],
+    [(0, 0), (1, 0), (-1, 0), (0, 1), (0, -1)],
 ]
 
 
@@ -275,7 +269,7 @@
             pltpu.SemaphoreType.DMA((hidden // NTILE + 1,)),
             pltpu.SemaphoreType.DMA((len(out_parts),)),
         ],
-        compiler_params=pltpu.CompilerParams(vmem_limit_bytes=50 << 20),
+        compiler_params=pltpu.CompilerParams(vmem_limit_bytes=(26 + 4 * nb) << 20),
         cost_estimate=pl.CostEstimate(flops=flops, bytes_accessed=moved, transcendentals=m * hidden),
     )(src, meta, *weights, *inputs)
     return [[v for v, part in zip(outs, out_parts) if part[0] == b] for b in range(nb)]

time: 317 us -> 316 us (level)
  Pallas kernels: 70.1 us -> 55 us
  starting transfers between devices: 68.3 us -> 57.3 us
  waiting for transfers between devices: 161 us -> 172 us
  local copies, waits for them, and re-layouts: 2.06 us -> 12.8 us
    ppermute x37 -> x35, waiting for transfers between devices: 113 us -> 131 us  [get_exp(): return lax.ppermute(x, 'exp', pairs)]
    pallas_call x5 -> x4, Pallas kernels: 70.1 us -> 55 us  [expert_blocks(): pl.pallas_call(functools.partial(expert_body, nb, parts, out_parts, piece...]
    ppermute x37 -> x35, starting transfers between devices: 57.2 us -> 42.7 us  [get_exp(): return lax.ppermute(x, 'exp', pairs)]
    unnamed x54 -> x78, local copies, waits for them, and re-layouts: 0.8 us -> 11.5 us
    ppermute x6, waiting for transfers between devices: 47.7 us -> 41.2 us  [get_x(): return lax.ppermute(v, 'grp', pairs)]
    add x4, other arithmetic: 0.03 us -> 4.9 us  [per_device(): src = ((me >> 2) + dz & 3) * 4 + (me + dy & 3)]
    convert_element_type x9, other arithmetic: 12.4 us -> 7.85 us  [add_up(): return total.astype(jnp.bfloat16)]
  transfers between devices with their start and end apart: 52 -> 50, of which waited for: 24 -> 20; matrix products, arithmetic and copies ran while one was open for 3% -> 5% of each run, Pallas kernels for 22% -> 18%
where the time goes in v2:
time: 316 us; the launch traced here: 313 us
  waiting for transfers between devices  172 us (54%)
  starting transfers between devices  57.3 us (18%)
  Pallas kernels  55 us (17%)
  other arithmetic  15.3 us (5%)
  local copies, waits for them, and re-layouts  12.8 us (4%)
    ppermute x35, waiting for transfers between devices, get_exp(): return lax.ppermute(x, 'exp', pairs)  131 us
    pallas_call x4, Pallas kernels, expert_blocks(): pl.pallas_call(functools.partial(expert_body, nb, parts, out_parts, piece...  55 us
    ppermute x35, starting transfers between devices, get_exp(): return lax.ppermute(x, 'exp', pairs)  42.7 us
    ppermute x6, waiting for transfers between devices, get_x(): return lax.ppermute(v, 'grp', pairs)  41.2 us
    unnamed x78, local copies, waits for them, and re-layouts  11.5 us
    ppermute x6, starting transfers between devices, get_x(): return lax.ppermute(v, 'grp', pairs)  9.48 us
    convert_element_type x9, other arithmetic, add_up(): return total.astype(jnp.bfloat16)  7.85 us
  transfers between devices with their start and end apart: 50, of which 20 were waited for; matrix products, arithmetic and copies ran while one was open for 5% of the time, Pallas kernels for 18%

profile of v2, /device:TPU:2, one launch (start us, length us, event | category | flops | bytes accessed | tf_op | source)
XLA Modules:
  0.0 313.1 jit_solution(8295620017262825585)
XLA Ops:
  6.1 4.0 %collective-permute-start.14 = (bf16[128,4096]{1,0:T(8,128)(2,1)S(1)}, bf16[128,4096]{1,0:T(8,128)(2,1)}, u32[]{:S(2)}, u32[]{:S(2)}) collective-permute-start(bf16[128,4096]{1,0:T(8,128)(2,1)S(1)} %copy-done.16), channel_id=1, source_target_pairs={{4,0},{5,1},{6,2},{7,3},{8,4},{9,5},{10,6},{11,7},{12,8},{13,9},{1... | collective-permute-start | bytes 3145736 | tf_op jit(solution)/shard_map/ppermute | solution.py:50
  11.8 14.6 %collective-permute-done.17.refs_20_ = bf16[128,4096]{1,0:T(8,128)(2,1)S(1)} collective-permute-done((bf16[128,4096]{1,0:T(8,128)(2,1)}, bf16[128,4096]{1,0:T(8,128)(2,1)S(1)}, u32[]{:S(2)}, u32[]{:S(2)}) %collective-permute-start.17) | collective-permute-done | bytes 1048608 | tf_op jit(solution)/shard_map/ppermute | solution.py:50
  32.8 6.4 %collective-permute-done.3.refs_5_ = bf16[144,4096]{1,0:T(8,128)(2,1)S(1)} collective-permute-done((bf16[144,4096]{1,0:T(8,128)(2,1)S(1)}, bf16[144,4096]{1,0:T(8,128)(2,1)S(1)}, u32[]{:S(2)}, u32[]{:S(2)}) %collective-permute-start.3) | collective-permute-done | bytes 1179680 | tf_op jit(solution)/shard_map/ppermute | solution.py:55
  39.2 23.6 %collective-permute-done.2.refs_4_ = bf16[144,4096]{1,0:T(8,128)(2,1)} collective-permute-done((bf16[144,4096]{1,0:T(8,128)(2,1)S(1)}, bf16[144,4096]{1,0:T(8,128)(2,1)}, u32[]{:S(2)}, u32[]{:S(2)}) %collective-permute-start.2) | collective-permute-done | bytes 1179680 | tf_op jit(solution)/shard_map/ppermute | solution.py:55
  62.8 2.8 collective-permute-start.4
  65.6 3.2 %collective-permute-start.20 = (bf16[128,4096]{1,0:T(8,128)(2,1)S(1)}, bf16[128,4096]{1,0:T(8,128)(2,1)}, u32[]{:S(2)}, u32[]{:S(2)}) collective-permute-start(bf16[128,4096]{1,0:T(8,128)(2,1)S(1)} %collective-permute-done.16.refs_19_), channel_id=1, source_target_pairs={{4,0},{5,1},{6,2},{7,3},{8,4},{9,5},{10,6},{11,7},{12,8},{13,9},{1... | collective-permute-start | bytes 3145736 | tf_op jit(solution)/shard_map/ppermute | solution.py:50
  68.8 10.0 %collective-permute-done.19.refs_17_ = bf16[64,4096]{1,0:T(8,128)(2,1)S(1)} collective-permute-done((bf16[64,4096]{1,0:T(8,128)(2,1)S(1)}, bf16[64,4096]{1,0:T(8,128)(2,1)S(1)}, u32[]{:S(2)}, u32[]{:S(2)}) %collective-permute-start.19) | collective-permute-done | bytes 524320 | tf_op jit(solution)/shard_map/ppermute | solution.py:50
  80.4 7.1 %collective-permute-done.23.refs_16_ = bf16[64,4096]{1,0:T(8,128)(2,1)} collective-permute-done((bf16[64,4096]{1,0:T(8,128)(2,1)S(1)}, bf16[64,4096]{1,0:T(8,128)(2,1)}, u32[]{:S(2)}, u32[]{:S(2)}) %collective-permute-start.23) | collective-permute-done | bytes 524320 | tf_op jit(solution)/shard_map/ppermute | solution.py:50
  90.9 11.2 %collective-permute-done.5.refs_7_ = bf16[144,4096]{1,0:T(8,128)(2,1)S(1)} collective-permute-done((bf16[144,4096]{1,0:T(8,128)(2,1)S(1)}, bf16[144,4096]{1,0:T(8,128)(2,1)S(1)}, u32[]{:S(2)}, u32[]{:S(2)}) %collective-permute-start.5) | collective-permute-done | bytes 1179680 | tf_op jit(solution)/shard_map/ppermute | solution.py:55
  102.1 2.9 collective-permute-start.32
  108.3 7.5 %collective-permute-done.29.refs_16_ = bf16[64,4096]{1,0:T(8,128)(2,1)} collective-permute-done((bf16[64,4096]{1,0:T(8,128)(2,1)}, bf16[64,4096]{1,0:T(8,128)(2,1)}, u32[]{:S(2)}, u32[]{:S(2)}) %collective-permute-start.29) | collective-permute-done | bytes 524320 | tf_op jit(solution)/shard_map/ppermute | solution.py:50
  115.8 1.9 collective-permute-start.30
  118.4 3.4 %all-to-all-start = ((f32[16,2,128]{2,1,0:T(2,128)}), f32[16,2,128]{2,1,0:T(2,128)S(1)}, u32[]{:S(2)}, u32[]{:S(2)}) async-start(f32[16,2,128]{2,1,0:T(2,128)} %pad_maximum_fusion.2), calls=%async_computation | async-start | bytes 32768 | tf_op jit(solution)/shard_map/all_to_all | solution.py:288
  123.1 7.9 %collective-permute-done.30.refs_17_ = bf16[64,4096]{1,0:T(8,128)(2,1)} collective-permute-done((bf16[64,4096]{1,0:T(8,128)(2,1)}, bf16[64,4096]{1,0:T(8,128)(2,1)}, u32[]{:S(2)}, u32[]{:S(2)}) %collective-permute-start.30) | collective-permute-done | bytes 524320 | tf_op jit(solution)/shard_map/ppermute | solution.py:50
  137.1 2.0 collective-permute-start.25
  144.7 11.9 %shard_map.139 = (bf16[64,4096]{1,0:T(8,128)(2,1)}, bf16[64,4096]{1,0:T(8,128)(2,1)}, bf16[128,4096]{1,0:T(8,128)(2,1)}, bf16[128,4096]{1,0:T(8,128)(2,1)S(1)}) custom-call(s32[3]{0:T(128)S(1)} %copy-done.12, f32[16,2,128]{2,1,0:T(2,128)S(1)} %all-to-all-done.meta_ref, bf16[144,4096]{1,0:T(8,128)(2,1)S(1)} %pad_maximum_fusion.refs_0_, ...), custom_call_target="tpu_custom_call" | custom-call | flops 5033164800 | bytes 25165824 | tf_op jit(solution)/shard_map/pallas_call | solution.py:250
  157.7 5.1 %collective-permute-done.24.refs_17_ = bf16[64,4096]{1,0:T(8,128)(2,1)} collective-permute-done((bf16[64,4096]{1,0:T(8,128)(2,1)}, bf16[64,4096]{1,0:T(8,128)(2,1)}, u32[]{:S(2)}, u32[]{:S(2)}) %collective-permute-start.24) | collective-permute-done | bytes 524320 | tf_op jit(solution)/shard_map/ppermute | solution.py:50
  164.9 13.4 %shard_map.138 = (bf16[128,4096]{1,0:T(8,128)(2,1)S(1)}, bf16[128,4096]{1,0:T(8,128)(2,1)S(1)}, bf16[128,4096]{1,0:T(8,128)(2,1)S(1)}, bf16[128,4096]{1,0:T(8,128)(2,1)S(1)}) custom-call(s32[4]{0:T(128)S(1)} %copy-done.14, f32[16,2,128]{2,1,0:T(2,128)S(1)} %all-to-all-done.meta_ref, bf16[144,4096]{1,0:T(8,128)(2,1)S(1)} %pad_maximum_fusion.refs_0_, ...), custom_call_target="tpu_custom_call" | custom-call | flops 6710886400 | bytes 27262976 | tf_op jit(solution)/shard_map/pallas_call | solution.py:250
  180.5 16.4 %shard_map.136 = (bf16[128,4096]{1,0:T(8,128)(2,1)S(1)}, bf16[128,4096]{1,0:T(8,128)(2,1)S(1)}, bf16[128,4096]{1,0:T(8,128)(2,1)S(1)}, bf16[128,4096]{1,0:T(8,128)(2,1)S(1)}, bf16[128,4096]{1,0:T(8,128)(2,1)S(1)}) custom-call(s32[5]{0:T(128)S(1)} %copy-done.15, f32[16,2,128]{2,1,0:T(2,128)S(1)} %all-to-all-done.meta_ref, bf16[144,4096]{1,0:T(8,128)(2,1)} %copy-done, ...), custom_call_target="tpu_custom_call" | custom-call | flops 8388608000 | bytes 29360128 | tf_op jit(solution)/shard_map/pallas_call | solution.py:250
  196.9 2.1 collective-permute-start.41
  201.0 13.2 %shard_map.137 = (bf16[128,4096]{1,0:T(8,128)(2,1)S(1)}, bf16[128,4096]{1,0:T(8,128)(2,1)S(1)}, bf16[128,4096]{1,0:T(8,128)(2,1)S(1)}, bf16[128,4096]{1,0:T(8,128)(2,1)S(1)}) custom-call(s32[4]{0:T(128)S(1)} %copy-done.13, f32[16,2,128]{2,1,0:T(2,128)S(1)} %all-to-all-done.meta_ref, bf16[144,4096]{1,0:T(8,128)(2,1)S(1)} %copy-done.1, ...), custom_call_target="tpu_custom_call" | custom-call | flops 6710886400 | bytes 27262976 | tf_op jit(solution)/shard_map/pallas_call | solution.py:250
  218.1 3.0 collective-permute-start.34
  221.1 3.1 collective-permute-done.41
  224.2 2.3 collective-permute-start.36
  228.2 30.3 %collective-permute-done.44 = bf16[128,4096]{1,0:T(8,128)(2,1)S(1)} collective-permute-done((bf16[128,4096]{1,0:T(8,128)(2,1)S(1)}, bf16[128,4096]{1,0:T(8,128)(2,1)S(1)}, u32[]{:S(2)}, u32[]{:S(2)}) %collective-permute-start.44) | collective-permute-done | bytes 1048608 | tf_op jit(solution)/shard_map/ppermute | solution.py:50
  259.6 2.4 collective-permute-start.45
  262.9 10.3 %collective-permute-done.47 = bf16[128,4096]{1,0:T(8,128)(2,1)S(1)} collective-permute-done((bf16[128,4096]{1,0:T(8,128)(2,1)S(1)}, bf16[128,4096]{1,0:T(8,128)(2,1)S(1)}, u32[]{:S(2)}, u32[]{:S(2)}) %collective-permute-start.47) | collective-permute-done | bytes 1048608 | tf_op jit(solution)/shard_map/ppermute | solution.py:50
  274.6 9.1 %collective-permute-done.42 = bf16[128,4096]{1,0:T(8,128)(2,1)S(1)} collective-permute-done((bf16[128,4096]{1,0:T(8,128)(2,1)S(1)}, bf16[128,4096]{1,0:T(8,128)(2,1)S(1)}, u32[]{:S(2)}, u32[]{:S(2)}) %collective-permute-start.42) | collective-permute-done | bytes 1048608 | tf_op jit(solution)/shard_map/ppermute | solution.py:50
  284.2 4.0 %collective-permute-start.43 = (bf16[128,4096]{1,0:T(8,128)(2,1)S(1)}, bf16[128,4096]{1,0:T(8,128)(2,1)S(1)}, u32[]{:S(2)}, u32[]{:S(2)}) collective-permute-start(bf16[128,4096]{1,0:T(8,128)(2,1)S(1)} %add_convert_fusion.3), channel_id=1, source_target_pairs={{3,0},{0,1},{1,2},{2,3},{7,4},{4,5},{5,6},{6,7},{11,8},{8,9},{9,10... | collective-permute-start | bytes 3145736 | tf_op jit(solution)/shard_map/ppermute | solution.py:50
  288.2 7.9 %collective-permute-done.37 = bf16[128,4096]{1,0:T(8,128)(2,1)S(1)} collective-permute-done((bf16[128,4096]{1,0:T(8,128)(2,1)S(1)}, bf16[128,4096]{1,0:T(8,128)(2,1)S(1)}, u32[]{:S(2)}, u32[]{:S(2)}) %collective-permute-start.37) | collective-permute-done | bytes 1048608 | tf_op jit(solution)/shard_map/ppermute | solution.py:50
  297.2 3.3 %collective-permute-done.43 = bf16[128,4096]{1,0:T(8,128)(2,1)S(1)} collective-permute-done((bf16[128,4096]{1,0:T(8,128)(2,1)S(1)}, bf16[128,4096]{1,0:T(8,128)(2,1)S(1)}, u32[]{:S(2)}, u32[]{:S(2)}) %collective-permute-start.43) | collective-permute-done | bytes 1048608 | tf_op jit(solution)/shard_map/ppermute | solution.py:50
  300.5 10.7 %collective-permute-done.38 = bf16[128,4096]{1,0:T(8,128)(2,1)S(1)} collective-permute-done((bf16[128,4096]{1,0:T(8,128)(2,1)S(1)}, bf16[128,4096]{1,0:T(8,128)(2,1)S(1)}, u32[]{:S(2)}, u32[]{:S(2)}) %collective-permute-start.38) | collective-permute-done | bytes 1048608 | tf_op jit(solution)/shard_map/ppermute | solution.py:50
  (174 shorter events, 55.5 us)
Async XLA Ops:
  0.0 26.4 %collective-permute-start.17 = (bf16[128,4096]{1,0:T(8,128)(2,1)}, bf16[128,4096]{1,0:T(8,128)(2,1)S(1)}, u32[]{:S(2)}, u32[]{:S(2)}) collective-permute-start(bf16[128,4096]{1,0:T(8,128)(2,1)} %refs_16_.1), channel_id=1, source_target_pairs={{3,0},{0,1},{1,2},{2,3},{7,4},{4,5},{5,6},{6,7},{11,8},{8,9},{9,10... | collective-permute-start | bytes 3145736 | tf_op jit(solution)/shard_map/ppermute | solution.py:50
  2.9 29.3 %collective-permute-start = (bf16[144,4096]{1,0:T(8,128)(2,1)S(1)}, bf16[144,4096]{1,0:T(8,128)(2,1)S(1)}, u32[]{:S(2)}, u32[]{:S(2)}) collective-permute-start(bf16[144,4096]{1,0:T(8,128)(2,1)S(1)} %pad_maximum_fusion.refs_0_), channel_id=1, source_target_pairs={{32,0},{48,16},{64,32},{80,48},{96,64},{112,80},{0,96},{16,112},{3... | collective-permute-start | bytes 3538952 | tf_op jit(solution)/shard_map/ppermute | solution.py:55
  6.1 26.1 %collective-permute-start.14 = (bf16[128,4096]{1,0:T(8,128)(2,1)S(1)}, bf16[128,4096]{1,0:T(8,128)(2,1)}, u32[]{:S(2)}, u32[]{:S(2)}) collective-permute-start(bf16[128,4096]{1,0:T(8,128)(2,1)S(1)} %copy-done.16), channel_id=1, source_target_pairs={{4,0},{5,1},{6,2},{7,3},{8,4},{9,5},{10,6},{11,7},{12,8},{13,9},{1... | collective-permute-start | bytes 3145736 | tf_op jit(solution)/shard_map/ppermute | solution.py:50
  10.3 28.9 %collective-permute-start.3 = (bf16[144,4096]{1,0:T(8,128)(2,1)S(1)}, bf16[144,4096]{1,0:T(8,128)(2,1)S(1)}, u32[]{:S(2)}, u32[]{:S(2)}) collective-permute-start(bf16[144,4096]{1,0:T(8,128)(2,1)S(1)} %pad_maximum_fusion.1.refs_1_), channel_id=1, source_target_pairs={{96,0},{112,16},{0,32},{16,48},{32,64},{48,80},{64,96},{80,112},{9... | collective-permute-start | bytes 3538952 | tf_op jit(solution)/shard_map/ppermute | solution.py:55
  26.4 36.4 %collective-permute-start.2 = (bf16[144,4096]{1,0:T(8,128)(2,1)S(1)}, bf16[144,4096]{1,0:T(8,128)(2,1)}, u32[]{:S(2)}, u32[]{:S(2)}) collective-permute-start(bf16[144,4096]{1,0:T(8,128)(2,1)S(1)} %pad_maximum_fusion.refs_0_), channel_id=1, source_target_pairs={{96,0},{112,16},{0,32},{16,48},{32,64},{48,80},{64,96},{80,112},{9... | collective-permute-start | bytes 3538952 | tf_op jit(solution)/shard_map/ppermute | solution.py:55
  29.0 33.8 %collective-permute-start.1 = (bf16[144,4096]{1,0:T(8,128)(2,1)S(1)}, bf16[144,4096]{1,0:T(8,128)(2,1)}, u32[]{:S(2)}, u32[]{:S(2)}) collective-permute-start(bf16[144,4096]{1,0:T(8,128)(2,1)S(1)} %pad_maximum_fusion.1.refs_1_), channel_id=1, source_target_pairs={{32,0},{48,16},{64,32},{80,48},{96,64},{112,80},{0,96},{16,112},{3... | collective-permute-start | bytes 3538952 | tf_op jit(solution)/shard_map/ppermute | solution.py:55
  32.2 33.4 %collective-permute-start.6 = (bf16[144,4096]{1,0:T(8,128)(2,1)S(1)}, bf16[144,4096]{1,0:T(8,128)(2,1)S(1)}, u32[]{:S(2)}, u32[]{:S(2)}) collective-permute-start(bf16[144,4096]{1,0:T(8,128)(2,1)S(1)} %pad_maximum_fusion.refs_0_), channel_id=1, source_target_pairs={{16,0},{0,16},{48,32},{32,48},{80,64},{64,80},{112,96},{96,112},{1... | collective-permute-start | bytes 3538952 | tf_op jit(solution)/shard_map/ppermute | solution.py:60
  32.2 46.7 %collective-permute-start.7 = (bf16[144,4096]{1,0:T(8,128)(2,1)S(1)}, bf16[144,4096]{1,0:T(8,128)(2,1)S(1)}, u32[]{:S(2)}, u32[]{:S(2)}) collective-permute-start(bf16[144,4096]{1,0:T(8,128)(2,1)S(1)} %pad_maximum_fusion.1.refs_1_), channel_id=1, source_target_pairs={{16,0},{0,16},{48,32},{32,48},{80,64},{64,80},{112,96},{96,112},{1... | collective-permute-start | bytes 3538952 | tf_op jit(solution)/shard_map/ppermute | solution.py:60
  39.2 29.6 %collective-permute-start.18 = (bf16[64,4096]{1,0:T(8,128)(2,1)S(1)}, bf16[64,4096]{1,0:T(8,128)(2,1)S(1)}, u32[]{:S(2)}, u32[]{:S(2)}) collective-permute-start(bf16[64,4096]{1,0:T(8,128)(2,1)S(1)} %get-tuple-element.40), channel_id=1, source_target_pairs={{12,0},{13,1},{14,2},{15,3},{0,4},{1,5},{2,6},{3,7},{4,8},{5,9},{6... | collective-permute-start | bytes 1572872 | tf_op jit(solution)/shard_map/ppermute | solution.py:50
  62.8 26.9 %collective-permute-start.4 = (bf16[144,4096]{1,0:T(8,128)(2,1)S(1)}, bf16[144,4096]{1,0:T(8,128)(2,1)S(1)}, u32[]{:S(2)}, u32[]{:S(2)}) collective-permute-start(bf16[144,4096]{1,0:T(8,128)(2,1)S(1)} %collective-permute-done.refs_2_), channel_id=1, source_target_pairs={{32,0},{48,16},{64,32},{80,48},{96,64},{112,80},{0,96},{16,112},{3... | collective-permute-start | bytes 3538952 | tf_op jit(solution)/shard_map/ppermute | solution.py:55
  102.1 30.5 %collective-permute-start.31 = (bf16[128,4096]{1,0:T(8,128)(2,1)}, bf16[128,4096]{1,0:T(8,128)(2,1)}, u32[]{:S(2)}, u32[]{:S(2)}) collective-permute-start(bf16[128,4096]{1,0:T(8,128)(2,1)} %collective-permute-done.20.refs_18_), channel_id=1, source_target_pairs={{4,0},{5,1},{6,2},{7,3},{8,4},{9,5},{10,6},{11,7},{12,8},{13,9},{1... | collective-permute-start | bytes 3145736 | tf_op jit(solution)/shard_map/ppermute | solution.py:50
  102.1 30.5 %collective-permute-start.32 = (bf16[128,4096]{1,0:T(8,128)(2,1)}, bf16[128,4096]{1,0:T(8,128)(2,1)}, u32[]{:S(2)}, u32[]{:S(2)}) collective-permute-start(bf16[128,4096]{1,0:T(8,128)(2,1)} %collective-permute-done.20.refs_18_), channel_id=1, source_target_pairs={{1,0},{2,1},{3,2},{0,3},{5,4},{6,5},{7,6},{4,7},{9,8},{10,9},{11,1... | collective-permute-start | bytes 3145736 | tf_op jit(solution)/shard_map/ppermute | solution.py:50
  107.1 29.6 %collective-permute-start.12 = (bf16[144,4096]{1,0:T(8,128)(2,1)}, bf16[144,4096]{1,0:T(8,128)(2,1)}, u32[]{:S(2)}, u32[]{:S(2)}) collective-permute-start(bf16[144,4096]{1,0:T(8,128)(2,1)} %copy-done.8), channel_id=1, source_target_pairs={{16,0},{0,16},{48,32},{32,48},{80,64},{64,80},{112,96},{96,112},{1... | collective-permute-start | bytes 3538952 | tf_op jit(solution)/shard_map/ppermute | solution.py:60
  107.2 29.9 %collective-permute-start.13 = (bf16[144,4096]{1,0:T(8,128)(2,1)}, bf16[144,4096]{1,0:T(8,128)(2,1)}, u32[]{:S(2)}, u32[]{:S(2)}) collective-permute-start(bf16[144,4096]{1,0:T(8,128)(2,1)} %copy-done.10), channel_id=1, source_target_pairs={{16,0},{0,16},{48,32},{32,48},{80,64},{64,80},{112,96},{96,112},{1... | collective-permute-start | bytes 3538952 | tf_op jit(solution)/shard_map/ppermute | solution.py:60
  131.0 26.7 %collective-permute-start.15 = (bf16[128,4096]{1,0:T(8,128)(2,1)}, bf16[128,4096]{1,0:T(8,128)(2,1)}, u32[]{:S(2)}, u32[]{:S(2)}) collective-permute-start(bf16[128,4096]{1,0:T(8,128)(2,1)} %refs_16_.1), channel_id=1, source_target_pairs={{12,0},{13,1},{14,2},{15,3},{0,4},{1,5},{2,6},{3,7},{4,8},{5,9},{6... | collective-permute-start | bytes 3145736 | tf_op jit(solution)/shard_map/ppermute | solution.py:50
  132.5 31.3 %collective-permute-start.28 = (bf16[128,4096]{1,0:T(8,128)(2,1)}, bf16[128,4096]{1,0:T(8,128)(2,1)}, u32[]{:S(2)}, u32[]{:S(2)}) collective-permute-start(bf16[128,4096]{1,0:T(8,128)(2,1)} %copy-done.38), channel_id=1, source_target_pairs={{1,0},{2,1},{3,2},{0,3},{5,4},{6,5},{7,6},{4,7},{9,8},{10,9},{11,1... | collective-permute-start | bytes 3145736 | tf_op jit(solution)/shard_map/ppermute | solution.py:50
  132.6 31.3 %collective-permute-start.27 = (bf16[128,4096]{1,0:T(8,128)(2,1)}, bf16[128,4096]{1,0:T(8,128)(2,1)}, u32[]{:S(2)}, u32[]{:S(2)}) collective-permute-start(bf16[128,4096]{1,0:T(8,128)(2,1)} %collective-permute-done.14.refs_17_), channel_id=1, source_target_pairs={{4,0},{5,1},{6,2},{7,3},{8,4},{9,5},{10,6},{11,7},{12,8},{13,9},{1... | collective-permute-start | bytes 3145736 | tf_op jit(solution)/shard_map/ppermute | solution.py:50
  136.7 26.1 %collective-permute-start.24 = (bf16[64,4096]{1,0:T(8,128)(2,1)}, bf16[64,4096]{1,0:T(8,128)(2,1)}, u32[]{:S(2)}, u32[]{:S(2)}) collective-permute-start(bf16[64,4096]{1,0:T(8,128)(2,1)} %copy-done.25), channel_id=1, source_target_pairs={{12,0},{13,1},{14,2},{15,3},{0,4},{1,5},{2,6},{3,7},{4,8},{5,9},{6... | collective-permute-start | bytes 1572872 | tf_op jit(solution)/shard_map/ppermute | solution.py:50
  137.1 25.7 %collective-permute-start.25 = (bf16[64,4096]{1,0:T(8,128)(2,1)}, bf16[64,4096]{1,0:T(8,128)(2,1)}, u32[]{:S(2)}, u32[]{:S(2)}) collective-permute-start(bf16[64,4096]{1,0:T(8,128)(2,1)} %copy-done.23), channel_id=1, source_target_pairs={{3,0},{0,1},{1,2},{2,3},{7,4},{4,5},{5,6},{6,7},{11,8},{8,9},{9,10... | collective-permute-start | bytes 1572872 | tf_op jit(solution)/shard_map/ppermute | solution.py:50
  157.7 39.2 %collective-permute-start.21 = (bf16[128,4096]{1,0:T(8,128)(2,1)}, bf16[128,4096]{1,0:T(8,128)(2,1)}, u32[]{:S(2)}, u32[]{:S(2)}) collective-permute-start(bf16[128,4096]{1,0:T(8,128)(2,1)} %collective-permute-done.14.refs_17_), channel_id=1, source_target_pairs={{3,0},{0,1},{1,2},{2,3},{7,4},{4,5},{5,6},{6,7},{11,8},{8,9},{9,10... | collective-permute-start | bytes 3145736 | tf_op jit(solution)/shard_map/ppermute | solution.py:50
  162.8 36.2 %collective-permute-start.22 = (bf16[128,4096]{1,0:T(8,128)(2,1)}, bf16[128,4096]{1,0:T(8,128)(2,1)}, u32[]{:S(2)}, u32[]{:S(2)}) collective-permute-start(bf16[128,4096]{1,0:T(8,128)(2,1)} %collective-permute-done.15.refs_18_), channel_id=1, source_target_pairs={{1,0},{2,1},{3,2},{0,3},{5,4},{6,5},{7,6},{4,7},{9,8},{10,9},{11,1... | collective-permute-start | bytes 3145736 | tf_op jit(solution)/shard_map/ppermute | solution.py:50
  162.8 51.4 %collective-permute-start.33 = (bf16[64,4096]{1,0:T(8,128)(2,1)}, bf16[64,4096]{1,0:T(8,128)(2,1)}, u32[]{:S(2)}, u32[]{:S(2)}) collective-permute-start(bf16[64,4096]{1,0:T(8,128)(2,1)} %get-tuple-element.26), channel_id=1, source_target_pairs={{4,0},{5,1},{6,2},{7,3},{8,4},{9,5},{10,6},{11,7},{12,8},{13,9},{1... | collective-permute-start | bytes 1572872 | tf_op jit(solution)/shard_map/ppermute | solution.py:50
  163.8 52.0 %collective-permute-start.35 = (bf16[64,4096]{1,0:T(8,128)(2,1)}, bf16[64,4096]{1,0:T(8,128)(2,1)}, u32[]{:S(2)}, u32[]{:S(2)}) collective-permute-start(bf16[64,4096]{1,0:T(8,128)(2,1)} %get-tuple-element.28), channel_id=1, source_target_pairs={{1,0},{2,1},{3,2},{0,3},{5,4},{6,5},{7,6},{4,7},{9,8},{10,9},{11,1... | collective-permute-start | bytes 1572872 | tf_op jit(solution)/shard_map/ppermute | solution.py:50
  163.9 54.2 %collective-permute-start.40 = (bf16[128,4096]{1,0:T(8,128)(2,1)}, bf16[128,4096]{1,0:T(8,128)(2,1)}, u32[]{:S(2)}, u32[]{:S(2)}) collective-permute-start(bf16[128,4096]{1,0:T(8,128)(2,1)} %get-tuple-element.32), channel_id=1, source_target_pairs={{12,0},{13,1},{14,2},{15,3},{0,4},{1,5},{2,6},{3,7},{4,8},{5,9},{6... | collective-permute-start | bytes 3145736 | tf_op jit(solution)/shard_map/ppermute | solution.py:50
  196.9 27.3 %collective-permute-start.41 = (bf16[128,4096]{1,0:T(8,128)(2,1)S(1)}, bf16[128,4096]{1,0:T(8,128)(2,1)S(1)}, u32[]{:S(2)}, u32[]{:S(2)}) collective-permute-start(bf16[128,4096]{1,0:T(8,128)(2,1)S(1)} %copy-done.20), channel_id=1, source_target_pairs={{3,0},{0,1},{1,2},{2,3},{7,4},{4,5},{5,6},{6,7},{11,8},{8,9},{9,10... | collective-permute-start | bytes 3145736 | tf_op jit(solution)/shard_map/ppermute | solution.py:50
  199.0 75.6 %collective-permute-start.39 = (bf16[128,4096]{1,0:T(8,128)(2,1)}, bf16[128,4096]{1,0:T(8,128)(2,1)S(1)}, u32[]{:S(2)}, u32[]{:S(2)}) collective-permute-start(bf16[128,4096]{1,0:T(8,128)(2,1)} %copy-done.18), channel_id=1, source_target_pairs={{3,0},{0,1},{1,2},{2,3},{7,4},{4,5},{5,6},{6,7},{11,8},{8,9},{9,10... | collective-permute-start | bytes 3145736 | tf_op jit(solution)/shard_map/ppermute | solution.py:50
  214.2 44.2 %collective-permute-start.44 = (bf16[128,4096]{1,0:T(8,128)(2,1)S(1)}, bf16[128,4096]{1,0:T(8,128)(2,1)S(1)}, u32[]{:S(2)}, u32[]{:S(2)}) collective-permute-start(bf16[128,4096]{1,0:T(8,128)(2,1)S(1)} %get-tuple-element.35), channel_id=1, source_target_pairs={{3,0},{0,1},{1,2},{2,3},{7,4},{4,5},{5,6},{6,7},{11,8},{8,9},{9,10... | collective-permute-start | bytes 3145736 | tf_op jit(solution)/shard_map/ppermute | solution.py:50
  216.0 46.5 %collective-permute-start.46 = (bf16[128,4096]{1,0:T(8,128)(2,1)S(1)}, bf16[128,4096]{1,0:T(8,128)(2,1)S(1)}, u32[]{:S(2)}, u32[]{:S(2)}) collective-permute-start(bf16[128,4096]{1,0:T(8,128)(2,1)S(1)} %copy-done.22), channel_id=1, source_target_pairs={{12,0},{13,1},{14,2},{15,3},{0,4},{1,5},{2,6},{3,7},{4,8},{5,9},{6... | collective-permute-start | bytes 3145736 | tf_op jit(solution)/shard_map/ppermute | solution.py:50
  218.1 40.6 %collective-permute-start.34 = (bf16[128,4096]{1,0:T(8,128)(2,1)S(1)}, bf16[128,4096]{1,0:T(8,128)(2,1)S(1)}, u32[]{:S(2)}, u32[]{:S(2)}) collective-permute-start(bf16[128,4096]{1,0:T(8,128)(2,1)S(1)} %add_convert_fusion.8), channel_id=1, source_target_pairs={{1,0},{2,1},{3,2},{0,3},{5,4},{6,5},{7,6},{4,7},{9,8},{10,9},{11,1... | collective-permute-start | bytes 3145736 | tf_op jit(solution)/shard_map/ppermute | solution.py:50
  224.2 35.4 %collective-permute-start.36 = (bf16[128,4096]{1,0:T(8,128)(2,1)S(1)}, bf16[128,4096]{1,0:T(8,128)(2,1)S(1)}, u32[]{:S(2)}, u32[]{:S(2)}) collective-permute-start(bf16[128,4096]{1,0:T(8,128)(2,1)S(1)} %add_convert_fusion.7), channel_id=1, source_target_pairs={{4,0},{5,1},{6,2},{7,3},{8,4},{9,5},{10,6},{11,7},{12,8},{13,9},{1... | collective-permute-start | bytes 3145736 | tf_op jit(solution)/shard_map/ppermute | solution.py:50
  259.6 36.9 %collective-permute-start.45 = (bf16[128,4096]{1,0:T(8,128)(2,1)S(1)}, bf16[128,4096]{1,0:T(8,128)(2,1)S(1)}, u32[]{:S(2)}, u32[]{:S(2)}) collective-permute-start(bf16[128,4096]{1,0:T(8,128)(2,1)S(1)} %add_convert_fusion.2), channel_id=1, source_target_pairs={{4,0},{5,1},{6,2},{7,3},{8,4},{9,5},{10,6},{11,7},{12,8},{13,9},{1... | collective-permute-start | bytes 3145736 | tf_op jit(solution)/shard_map/ppermute | solution.py:50
  262.5 33.7 %collective-permute-start.37 = (bf16[128,4096]{1,0:T(8,128)(2,1)S(1)}, bf16[128,4096]{1,0:T(8,128)(2,1)S(1)}, u32[]{:S(2)}, u32[]{:S(2)}) collective-permute-start(bf16[128,4096]{1,0:T(8,128)(2,1)S(1)} %add_convert_fusion.6), channel_id=1, source_target_pairs={{4,0},{5,1},{6,2},{7,3},{8,4},{9,5},{10,6},{11,7},{12,8},{13,9},{1... | collective-permute-start | bytes 3145736 | tf_op jit(solution)/shard_map/ppermute | solution.py:50
  (57 other events, 1409.9 us)

commit v3 on v2

--- a/solution.py
+++ b/solution.py
@@ -33,12 +33,13 @@
 }
 
 BACK = {o: [(0, 128) + parts[0][2:]] for o, parts in TREE.items()}
-BACK[2, 2] = TREE[2, 2]
+for split in ((2, 2), (2, -1), (-1, 2), (-1, -1)):
+    BACK[split] = TREE[split]
 
 BATCHES = [
     [(2, 2), (2, 1), (1, 2)],
-    [(2, -1), (-1, 2), (2, 0), (0, 2)],
-    [(-1, -1), (1, 1), (1, -1), (-1, 1)],
+    [(2, -1), (-1, 2), (1, 1), (0, 2)],
+    [(-1, -1), (2, 0), (1, -1), (-1, 1)],
     [(0, 0), (1, 0), (-1, 0), (0, 1), (0, -1)],
 ]
 
@@ -114,11 +115,17 @@
 def reduce_back(partial):
     extra = {offset: [] for offset in partial}
     for offset, parts in reversed(BACK.items()):
-        values = partial[offset]
-        if extra[offset]:
-            values = [add_up(values[0], extra[offset])]
         for i, (row, rows, way, before) in enumerate(parts):
-            extra[before].append((row, get_exp(values[i], -way[0], -way[1])))
+            value = partial[offset][i]
+            mine = [
+                (at - row, v)
+                for at, v in extra[offset]
+                if at < row + rows and row < at + v.shape[0]
+            ]
+            assert all(at >= 0 and at + v.shape[0] <= rows for at, v in mine)
+            if mine:
+                value = add_up(value, mine)
+            extra[before].append((row, get_exp(value, -way[0], -way[1])))
     return add_up(partial[0, 0][0], extra[0, 0])
 
 
@@ -144,7 +151,7 @@
     return pieces
 
 
-def expert_body(nb, parts, out_parts, pieces, src_ref, meta_ref, *refs):
+def expert_body(base, nb, parts, out_parts, pieces, src_ref, meta_ref, *refs):
     weights, refs = refs[:16], refs[16:]
     inputs, refs = refs[: len(parts)], refs[len(parts) :]
     outs, refs = refs[: len(out_parts)], refs[len(out_parts) :]
@@ -175,7 +182,7 @@
 
     @pl.loop(0, nb)
     def _(b):
-        source = src_ref[b]
+        source = src_ref[base + b]
         hit = jnp.where(slots == meta_ref[source, 0:1, :], 1.0, 0.0)
         scale = jnp.sum(hit * meta_ref[source, 1:2, :], axis=1, keepdims=True)
         rows = pl.ds(pl.multiple_of(b * CAP, CAP), CAP)
@@ -229,7 +236,7 @@
         out_copy(i).wait()
 
 
-def expert_blocks(src, meta, blocks, weights, cuts):
+def expert_blocks(src, base, meta, blocks, weights, cuts):
     nb = len(blocks)
     parts, inputs = [], []
     for b, block in enumerate(blocks):
@@ -248,7 +255,7 @@
     flops = 2 * m * width * hidden * 3 + 4 * m * rows * width
     moved = 2 * (3 * hidden * width + 2 * nb * rows * width)
     outs = pl.pallas_call(
-        functools.partial(expert_body, nb, parts, out_parts, pieces),
+        functools.partial(expert_body, base, nb, parts, out_parts, pieces),
         out_shape=[jax.ShapeDtypeStruct((part[2], width), jnp.bfloat16) for part in out_parts],
         in_specs=[
             pl.BlockSpec(memory_space=pltpu.SMEM),
@@ -288,13 +295,15 @@
     meta = lax.all_to_all(meta, "exp", split_axis=0, concat_axis=0, tiled=True)
 
     partial = {}
+    dz = jnp.array([o[0] for batch in BATCHES for o in batch], jnp.int32)
+    dy = jnp.array([o[1] for batch in BATCHES for o in batch], jnp.int32)
+    src = (((me >> 2) + dz) & 3) * 4 + ((me + dy) & 3)
+    base = 0
     for batch in BATCHES:
-        dz = jnp.array([o[0] for o in batch], jnp.int32)
-        dy = jnp.array([o[1] for o in batch], jnp.int32)
-        src = (((me >> 2) + dz) & 3) * 4 + ((me + dy) & 3)
         cuts = [[part[:2] for part in BACK.get(o, [(0, 128)])] for o in batch]
-        outs = expert_blocks(src, meta, [blocks[o] for o in batch], weights, cuts)
+        outs = expert_blocks(src, base, meta, [blocks[o] for o in batch], weights, cuts)
         partial.update(zip(batch, outs))
+        base += len(batch)
     return reduce_back(partial)
 
 

time: 316 us -> 372 us (1.18)
  waiting for transfers between devices: 172 us -> 218 us
  starting transfers between devices: 57.3 us -> 67.7 us
  local copies, waits for them, and re-layouts: 12.8 us -> 17.1 us
    ppermute x35 -> x38, waiting for transfers between devices: 131 us -> 161 us  [get_exp(): return lax.ppermute(x, 'exp', pairs)]
    all_to_all x1, waiting for transfers between devices: 0.01 us -> 14.2 us  [per_device(): meta = lax.all_to_all(meta, 'exp', split_axis=0, concat_axis=0, tiled=True)]
    ppermute x35 -> x38, starting transfers between devices: 42.7 us -> 54.2 us  [get_exp(): return lax.ppermute(x, 'exp', pairs)]
    unnamed x78 -> x84, local copies, waits for them, and re-layouts: 11.5 us -> 15.8 us
    convert_element_type x9 -> x10, other arithmetic: 7.85 us -> 8.16 us  [add_up(): return total.astype(jnp.bfloat16)]
  transfers between devices with their start and end apart: 50 -> 53, of which waited for: 20 -> 20; matrix products, arithmetic and copies ran while one was open for 5% -> 3% of each run, Pallas kernels for 18% -> 15%
where the time goes in v3:
time: 372 us; the launch traced here: 369 us
  waiting for transfers between devices  218 us (59%)
  starting transfers between devices  67.7 us (18%)
  Pallas kernels  54.4 us (15%)
  local copies, waits for them, and re-layouts  17.1 us (5%)
  other arithmetic  11.9 us (3%)
    ppermute x38, waiting for transfers between devices, get_exp(): return lax.ppermute(x, 'exp', pairs)  161 us
    pallas_call x4, Pallas kernels, expert_blocks(): pl.pallas_call(functools.partial(expert_body, base, nb, parts, out_parts,...  54.4 us
    ppermute x38, starting transfers between devices, get_exp(): return lax.ppermute(x, 'exp', pairs)  54.2 us
    ppermute x6, waiting for transfers between devices, get_x(): return lax.ppermute(v, 'grp', pairs)  43 us
    unnamed x84, local copies, waits for them, and re-layouts  15.8 us
    all_to_all x1, waiting for transfers between devices, per_device(): meta = lax.all_to_all(meta, 'exp', split_axis=0, concat_axis=0, tiled=True)  14.2 us
    convert_element_type x10, other arithmetic, add_up(): return total.astype(jnp.bfloat16)  8.16 us
  transfers between devices with their start and end apart: 53, of which 20 were waited for; matrix products, arithmetic and copies ran while one was open for 3% of the time, Pallas kernels for 15%

profile of v3, /device:TPU:2, one launch (start us, length us, event | category | flops | bytes accessed | tf_op | source)
XLA Modules:
  0.0 369.4 jit_solution(13326964026589764069)
XLA Ops:
  1.6 4.0 %collective-permute-start.14 = (bf16[128,4096]{1,0:T(8,128)(2,1)}, bf16[128,4096]{1,0:T(8,128)(2,1)S(1)}, u32[]{:S(2)}, u32[]{:S(2)}) collective-permute-start(bf16[128,4096]{1,0:T(8,128)(2,1)} %refs_16_.1), channel_id=1, source_target_pairs={{4,0},{5,1},{6,2},{7,3},{8,4},{9,5},{10,6},{11,7},{12,8},{13,9},{1... | collective-permute-start | bytes 3145736 | tf_op jit(solution)/shard_map/ppermute | solution.py:51
  10.0 16.4 %collective-permute-done.17.refs_20_ = bf16[128,4096]{1,0:T(8,128)(2,1)S(1)} collective-permute-done((bf16[128,4096]{1,0:T(8,128)(2,1)}, bf16[128,4096]{1,0:T(8,128)(2,1)S(1)}, u32[]{:S(2)}, u32[]{:S(2)}) %collective-permute-start.17) | collective-permute-done | bytes 1048608 | tf_op jit(solution)/shard_map/ppermute | solution.py:51
  32.9 4.6 %collective-permute-done.refs_2_ = bf16[144,4096]{1,0:T(8,128)(2,1)S(1)} collective-permute-done((bf16[144,4096]{1,0:T(8,128)(2,1)S(1)}, bf16[144,4096]{1,0:T(8,128)(2,1)S(1)}, u32[]{:S(2)}, u32[]{:S(2)}) %collective-permute-start) | collective-permute-done | bytes 1179680 | tf_op jit(solution)/shard_map/ppermute | solution.py:56
  37.5 23.5 %collective-permute-done.1.refs_3_ = bf16[144,4096]{1,0:T(8,128)(2,1)} collective-permute-done((bf16[144,4096]{1,0:T(8,128)(2,1)S(1)}, bf16[144,4096]{1,0:T(8,128)(2,1)}, u32[]{:S(2)}, u32[]{:S(2)}) %collective-permute-start.1) | collective-permute-done | bytes 1179680 | tf_op jit(solution)/shard_map/ppermute | solution.py:56
  61.0 3.0 collective-permute-start.20
  65.2 14.8 %collective-permute-done.3.refs_5_ = bf16[144,4096]{1,0:T(8,128)(2,1)} collective-permute-done((bf16[144,4096]{1,0:T(8,128)(2,1)S(1)}, bf16[144,4096]{1,0:T(8,128)(2,1)}, u32[]{:S(2)}, u32[]{:S(2)}) %collective-permute-start.3) | collective-permute-done | bytes 1179680 | tf_op jit(solution)/shard_map/ppermute | solution.py:56
  85.7 13.0 %collective-permute-done.18.refs_16_ = bf16[64,4096]{1,0:T(8,128)(2,1)S(1)} collective-permute-done((bf16[64,4096]{1,0:T(8,128)(2,1)S(1)}, bf16[64,4096]{1,0:T(8,128)(2,1)S(1)}, u32[]{:S(2)}, u32[]{:S(2)}) %collective-permute-start.18) | collective-permute-done | bytes 524320 | tf_op jit(solution)/shard_map/ppermute | solution.py:51
  98.6 11.2 %collective-permute-done.19.refs_17_ = bf16[64,4096]{1,0:T(8,128)(2,1)S(1)} collective-permute-done((bf16[64,4096]{1,0:T(8,128)(2,1)S(1)}, bf16[64,4096]{1,0:T(8,128)(2,1)S(1)}, u32[]{:S(2)}, u32[]{:S(2)}) %collective-permute-start.19) | collective-permute-done | bytes 524320 | tf_op jit(solution)/shard_map/ppermute | solution.py:51
  109.9 3.0 collective-permute-start.4
  116.0 2.0 collective-permute-start.27
  118.7 14.6 %collective-permute-done.26.refs_19_ = bf16[64,4096]{1,0:T(8,128)(2,1)S(1)} collective-permute-done((bf16[64,4096]{1,0:T(8,128)(2,1)S(1)}, bf16[64,4096]{1,0:T(8,128)(2,1)S(1)}, u32[]{:S(2)}, u32[]{:S(2)}) %collective-permute-start.26) | collective-permute-done | bytes 524320 | tf_op jit(solution)/shard_map/ppermute | solution.py:51
  133.3 8.3 %collective-permute-done.27.refs_20_ = bf16[128,4096]{1,0:T(8,128)(2,1)S(1)} collective-permute-done((bf16[128,4096]{1,0:T(8,128)(2,1)S(1)}, bf16[128,4096]{1,0:T(8,128)(2,1)S(1)}, u32[]{:S(2)}, u32[]{:S(2)}) %collective-permute-start.27) | collective-permute-done | bytes 1048608 | tf_op jit(solution)/shard_map/ppermute | solution.py:51
  147.4 5.7 %all-to-all-start = ((f32[16,2,128]{2,1,0:T(2,128)}), f32[16,2,128]{2,1,0:T(2,128)S(1)}, u32[]{:S(2)}, u32[]{:S(2)}) async-start(f32[16,2,128]{2,1,0:T(2,128)} %pad_maximum_fusion.2), calls=%async_computation | async-start | bytes 32768 | tf_op jit(solution)/shard_map/all_to_all | solution.py:295
  160.8 14.2 %all-to-all-done.meta_ref = f32[16,2,128]{2,1,0:T(2,128)S(1)} async-done(((f32[16,2,128]{2,1,0:T(2,128)}), f32[16,2,128]{2,1,0:T(2,128)S(1)}, u32[]{:S(2)}, u32[]{:S(2)}) %all-to-all-start) | async-done | bytes 16416 | tf_op jit(solution)/shard_map/all_to_all | solution.py:295
  181.4 13.8 %shard_map.83 = (bf16[64,4096]{1,0:T(8,128)(2,1)S(1)}, bf16[64,4096]{1,0:T(8,128)(2,1)S(1)}, bf16[128,4096]{1,0:T(8,128)(2,1)}, bf16[128,4096]{1,0:T(8,128)(2,1)}, bf16[128,4096]{1,0:T(8,128)(2,1)S(1)}) custom-call(s32[16]{0:T(128)S(1)} %copy-done.3, f32[16,2,128]{2,1,0:T(2,128)S(1)} %all-to-all-done.meta_ref, ...), custom_call_target="tpu_custom_call" | custom-call | flops 6710886400 | bytes 27262976 | tf_op jit(solution)/shard_map/pallas_call | solution.py:257
  196.5 2.9 collective-permute-start.50
  199.4 13.3 %shard_map.84 = (bf16[64,4096]{1,0:T(8,128)(2,1)S(1)}, bf16[64,4096]{1,0:T(8,128)(2,1)}, bf16[64,4096]{1,0:T(8,128)(2,1)S(1)}, bf16[64,4096]{1,0:T(8,128)(2,1)S(...) custom-call(s32[16]{0:T(128)S(1)} %copy-done.3, f32[16,2,128]{2,1,0:T(2,128)S(1)} %all-to-all-done.meta_ref, ...), custom_call_target="tpu_custom_call" | custom-call | flops 6710886400 | bytes 27262976 | tf_op jit(solution)/shard_map/pallas_call | solution.py:257
  213.4 2.7 collective-permute-start.39
  216.2 11.4 %shard_map.85 = (bf16[64,4096]{1,0:T(8,128)(2,1)S(1)}, bf16[64,4096]{1,0:T(8,128)(2,1)}, bf16[128,4096]{1,0:T(8,128)(2,1)S(1)}, bf16[128,4096]{1,0:T(8,128)(2,1)S(1)}) custom-call(s32[16]{0:T(128)S(1)} %copy-done.4, f32[16,2,128]{2,1,0:T(2,128)S(1)} %all-to-all-done.meta_ref, bf16[144,4096]{1,0:T(8,128)(2,1)S(1)} %pad_maximum_fusion.refs_0_, ...), custom_call_target="tpu_custom_call" | custom-call | flops 5033164800 | bytes 25165824 | tf_op jit(solution)/shard_map/pallas_call | solution.py:257
  231.6 15.8 %shard_map.82 = (bf16[128,4096]{1,0:T(8,128)(2,1)S(1)}, bf16[128,4096]{1,0:T(8,128)(2,1)S(1)}, bf16[128,4096]{1,0:T(8,128)(2,1)S(1)}, bf16[128,4096]{1,0:T(8,128)(2,1)S(1)}, bf16[128,4096]{1,0:T(8,128)(2,1)S(1)}) custom-call(s32[16]{0:T(128)S(1)} %copy-done.4, f32[16,2,128]{2,1,0:T(2,128)S(1)} %all-to-all-done.meta_ref, bf16[144,4096]{1,0:T(8,128)(2,1)} %copy-done, ...), custom_call_target="tpu_custom_call" | custom-call | flops 8388608000 | bytes 29360128 | tf_op jit(solution)/shard_map/pallas_call | solution.py:257
  247.4 3.2 collective-permute-start.34
  250.8 8.7 %collective-permute-done.34 = bf16[64,4096]{1,0:T(8,128)(2,1)S(1)} collective-permute-done((bf16[64,4096]{1,0:T(8,128)(2,1)S(1)}, bf16[64,4096]{1,0:T(8,128)(2,1)S(1)}, u32[]{:S(2)}, u32[]{:S(2)}) %collective-permute-start.34) | collective-permute-done | bytes 524320 | tf_op jit(solution)/shard_map/ppermute | solution.py:51
  259.5 3.2 collective-permute-start.38
  263.0 11.9 %collective-permute-done.38 = bf16[64,4096]{1,0:T(8,128)(2,1)S(1)} collective-permute-done((bf16[64,4096]{1,0:T(8,128)(2,1)S(1)}, bf16[64,4096]{1,0:T(8,128)(2,1)S(1)}, u32[]{:S(2)}, u32[]{:S(2)}) %collective-permute-start.38) | collective-permute-done | bytes 524320 | tf_op jit(solution)/shard_map/ppermute | solution.py:51
  276.3 4.2 %collective-permute-done.29 = bf16[64,4096]{1,0:T(8,128)(2,1)S(1)} collective-permute-done((bf16[64,4096]{1,0:T(8,128)(2,1)S(1)}, bf16[64,4096]{1,0:T(8,128)(2,1)S(1)}, u32[]{:S(2)}, u32[]{:S(2)}) %collective-permute-start.29) | collective-permute-done | bytes 524320 | tf_op jit(solution)/shard_map/ppermute | solution.py:51
  281.0 6.9 %collective-permute-done.35 = bf16[64,4096]{1,0:T(8,128)(2,1)S(1)} collective-permute-done((bf16[64,4096]{1,0:T(8,128)(2,1)S(1)}, bf16[64,4096]{1,0:T(8,128)(2,1)S(1)}, u32[]{:S(2)}, u32[]{:S(2)}) %collective-permute-start.35) | collective-permute-done | bytes 524320 | tf_op jit(solution)/shard_map/ppermute | solution.py:51
  293.5 14.6 %collective-permute-done.44 = bf16[128,4096]{1,0:T(8,128)(2,1)S(1)} collective-permute-done((bf16[128,4096]{1,0:T(8,128)(2,1)S(1)}, bf16[128,4096]{1,0:T(8,128)(2,1)S(1)}, u32[]{:S(2)}, u32[]{:S(2)}) %collective-permute-start.44) | collective-permute-done | bytes 1048608 | tf_op jit(solution)/shard_map/ppermute | solution.py:51
  313.1 2.4 collective-permute-start.48
  315.5 5.9 %collective-permute-done.36 = bf16[64,4096]{1,0:T(8,128)(2,1)S(1)} collective-permute-done((bf16[64,4096]{1,0:T(8,128)(2,1)S(1)}, bf16[64,4096]{1,0:T(8,128)(2,1)S(1)}, u32[]{:S(2)}, u32[]{:S(2)}) %collective-permute-start.36) | collective-permute-done | bytes 524320 | tf_op jit(solution)/shard_map/ppermute | solution.py:51
  321.7 3.6 collective-permute-start.41
  325.3 23.5 %collective-permute-done.45 = bf16[128,4096]{1,0:T(8,128)(2,1)S(1)} collective-permute-done((bf16[128,4096]{1,0:T(8,128)(2,1)S(1)}, bf16[128,4096]{1,0:T(8,128)(2,1)S(1)}, u32[]{:S(2)}, u32[]{:S(2)}) %collective-permute-start.45) | collective-permute-done | bytes 1048608 | tf_op jit(solution)/shard_map/ppermute | solution.py:51
  349.4 18.1 %collective-permute-done.46 = bf16[128,4096]{1,0:T(8,128)(2,1)S(1)} collective-permute-done((bf16[128,4096]{1,0:T(8,128)(2,1)S(1)}, bf16[128,4096]{1,0:T(8,128)(2,1)S(1)}, u32[]{:S(2)}, u32[]{:S(2)}) %collective-permute-start.46) | collective-permute-done | bytes 1048608 | tf_op jit(solution)/shard_map/ppermute | solution.py:51
  (184 shorter events, 64.2 us)
Async XLA Ops:
  0.0 26.4 %collective-permute-start.17 = (bf16[128,4096]{1,0:T(8,128)(2,1)}, bf16[128,4096]{1,0:T(8,128)(2,1)S(1)}, u32[]{:S(2)}, u32[]{:S(2)}) collective-permute-start(bf16[128,4096]{1,0:T(8,128)(2,1)} %refs_16_.1), channel_id=1, source_target_pairs={{3,0},{0,1},{1,2},{2,3},{7,4},{4,5},{5,6},{6,7},{11,8},{8,9},{9,10... | collective-permute-start | bytes 3145736 | tf_op jit(solution)/shard_map/ppermute | solution.py:51
  1.6 26.5 %collective-permute-start.14 = (bf16[128,4096]{1,0:T(8,128)(2,1)}, bf16[128,4096]{1,0:T(8,128)(2,1)S(1)}, u32[]{:S(2)}, u32[]{:S(2)}) collective-permute-start(bf16[128,4096]{1,0:T(8,128)(2,1)} %refs_16_.1), channel_id=1, source_target_pairs={{4,0},{5,1},{6,2},{7,3},{8,4},{9,5},{10,6},{11,7},{12,8},{13,9},{1... | collective-permute-start | bytes 3145736 | tf_op jit(solution)/shard_map/ppermute | solution.py:51
  5.6 27.3 %collective-permute-start.16 = (bf16[128,4096]{1,0:T(8,128)(2,1)}, bf16[128,4096]{1,0:T(8,128)(2,1)S(1)}, u32[]{:S(2)}, u32[]{:S(2)}) collective-permute-start(bf16[128,4096]{1,0:T(8,128)(2,1)} %refs_16_.1), channel_id=1, source_target_pairs={{1,0},{2,1},{3,2},{0,3},{5,4},{6,5},{7,6},{4,7},{9,8},{10,9},{11,1... | collective-permute-start | bytes 3145736 | tf_op jit(solution)/shard_map/ppermute | solution.py:51
  8.6 28.9 %collective-permute-start = (bf16[144,4096]{1,0:T(8,128)(2,1)S(1)}, bf16[144,4096]{1,0:T(8,128)(2,1)S(1)}, u32[]{:S(2)}, u32[]{:S(2)}) collective-permute-start(bf16[144,4096]{1,0:T(8,128)(2,1)S(1)} %pad_maximum_fusion.refs_0_), channel_id=1, source_target_pairs={{32,0},{48,16},{64,32},{80,48},{96,64},{112,80},{0,96},{16,112},{3... | collective-permute-start | bytes 3538952 | tf_op jit(solution)/shard_map/ppermute | solution.py:56
  26.4 34.6 %collective-permute-start.1 = (bf16[144,4096]{1,0:T(8,128)(2,1)S(1)}, bf16[144,4096]{1,0:T(8,128)(2,1)}, u32[]{:S(2)}, u32[]{:S(2)}) collective-permute-start(bf16[144,4096]{1,0:T(8,128)(2,1)S(1)} %pad_maximum_fusion.1.refs_1_), channel_id=1, source_target_pairs={{32,0},{48,16},{64,32},{80,48},{96,64},{112,80},{0,96},{16,112},{3... | collective-permute-start | bytes 3538952 | tf_op jit(solution)/shard_map/ppermute | solution.py:56
  28.1 35.9 %collective-permute-start.2 = (bf16[144,4096]{1,0:T(8,128)(2,1)S(1)}, bf16[144,4096]{1,0:T(8,128)(2,1)}, u32[]{:S(2)}, u32[]{:S(2)}) collective-permute-start(bf16[144,4096]{1,0:T(8,128)(2,1)S(1)} %pad_maximum_fusion.refs_0_), channel_id=1, source_target_pairs={{96,0},{112,16},{0,32},{16,48},{32,64},{48,80},{64,96},{80,112},{9... | collective-permute-start | bytes 3538952 | tf_op jit(solution)/shard_map/ppermute | solution.py:56
  31.4 48.6 %collective-permute-start.3 = (bf16[144,4096]{1,0:T(8,128)(2,1)S(1)}, bf16[144,4096]{1,0:T(8,128)(2,1)}, u32[]{:S(2)}, u32[]{:S(2)}) collective-permute-start(bf16[144,4096]{1,0:T(8,128)(2,1)S(1)} %pad_maximum_fusion.1.refs_1_), channel_id=1, source_target_pairs={{96,0},{112,16},{0,32},{16,48},{32,64},{48,80},{64,96},{80,112},{9... | collective-permute-start | bytes 3538952 | tf_op jit(solution)/shard_map/ppermute | solution.py:56
  32.9 49.2 %collective-permute-start.6 = (bf16[144,4096]{1,0:T(8,128)(2,1)S(1)}, bf16[144,4096]{1,0:T(8,128)(2,1)S(1)}, u32[]{:S(2)}, u32[]{:S(2)}) collective-permute-start(bf16[144,4096]{1,0:T(8,128)(2,1)S(1)} %pad_maximum_fusion.refs_0_), channel_id=1, source_target_pairs={{16,0},{0,16},{48,32},{32,48},{80,64},{64,80},{112,96},{96,112},{1... | collective-permute-start | bytes 3538952 | tf_op jit(solution)/shard_map/ppermute | solution.py:61
  37.5 46.2 %collective-permute-start.7 = (bf16[144,4096]{1,0:T(8,128)(2,1)S(1)}, bf16[144,4096]{1,0:T(8,128)(2,1)S(1)}, u32[]{:S(2)}, u32[]{:S(2)}) collective-permute-start(bf16[144,4096]{1,0:T(8,128)(2,1)S(1)} %pad_maximum_fusion.1.refs_1_), channel_id=1, source_target_pairs={{16,0},{0,16},{48,32},{32,48},{80,64},{64,80},{112,96},{96,112},{1... | collective-permute-start | bytes 3538952 | tf_op jit(solution)/shard_map/ppermute | solution.py:61
  61.0 51.8 %collective-permute-start.20 = (bf16[128,4096]{1,0:T(8,128)(2,1)S(1)}, bf16[128,4096]{1,0:T(8,128)(2,1)S(1)}, u32[]{:S(2)}, u32[]{:S(2)}) collective-permute-start(bf16[128,4096]{1,0:T(8,128)(2,1)S(1)} %collective-permute-done.14.refs_17_), channel_id=1, source_target_pairs={{4,0},{5,1},{6,2},{7,3},{8,4},{9,5},{10,6},{11,7},{12,8},{13,9},{1... | collective-permute-start | bytes 3145736 | tf_op jit(solution)/shard_map/ppermute | solution.py:51
  64.0 49.8 %collective-permute-start.21 = (bf16[128,4096]{1,0:T(8,128)(2,1)S(1)}, bf16[128,4096]{1,0:T(8,128)(2,1)S(1)}, u32[]{:S(2)}, u32[]{:S(2)}) collective-permute-start(bf16[128,4096]{1,0:T(8,128)(2,1)S(1)} %collective-permute-done.14.refs_17_), channel_id=1, source_target_pairs={{3,0},{0,1},{1,2},{2,3},{7,4},{4,5},{5,6},{6,7},{11,8},{8,9},{9,10... | collective-permute-start | bytes 3145736 | tf_op jit(solution)/shard_map/ppermute | solution.py:51
  80.0 34.9 %collective-permute-start.22 = (bf16[128,4096]{1,0:T(8,128)(2,1)S(1)}, bf16[128,4096]{1,0:T(8,128)(2,1)S(1)}, u32[]{:S(2)}, u32[]{:S(2)}) collective-permute-start(bf16[128,4096]{1,0:T(8,128)(2,1)S(1)} %collective-permute-done.15.refs_18_), channel_id=1, source_target_pairs={{1,0},{2,1},{3,2},{0,3},{5,4},{6,5},{7,6},{4,7},{9,8},{10,9},{11,1... | collective-permute-start | bytes 3145736 | tf_op jit(solution)/shard_map/ppermute | solution.py:51
  83.8 26.1 %collective-permute-start.19 = (bf16[64,4096]{1,0:T(8,128)(2,1)S(1)}, bf16[64,4096]{1,0:T(8,128)(2,1)S(1)}, u32[]{:S(2)}, u32[]{:S(2)}) collective-permute-start(bf16[64,4096]{1,0:T(8,128)(2,1)S(1)} %get-tuple-element.45), channel_id=1, source_target_pairs={{12,0},{13,1},{14,2},{15,3},{0,4},{1,5},{2,6},{3,7},{4,8},{5,9},{6... | collective-permute-start | bytes 1572872 | tf_op jit(solution)/shard_map/ppermute | solution.py:51
  109.9 31.7 %collective-permute-start.4 = (bf16[144,4096]{1,0:T(8,128)(2,1)S(1)}, bf16[144,4096]{1,0:T(8,128)(2,1)}, u32[]{:S(2)}, u32[]{:S(2)}) collective-permute-start(bf16[144,4096]{1,0:T(8,128)(2,1)S(1)} %collective-permute-done.refs_2_), channel_id=1, source_target_pairs={{32,0},{48,16},{64,32},{80,48},{96,64},{112,80},{0,96},{16,112},{3... | collective-permute-start | bytes 3538952 | tf_op jit(solution)/shard_map/ppermute | solution.py:56
  113.8 28.2 %collective-permute-start.5 = (bf16[144,4096]{1,0:T(8,128)(2,1)}, bf16[144,4096]{1,0:T(8,128)(2,1)}, u32[]{:S(2)}, u32[]{:S(2)}) collective-permute-start(bf16[144,4096]{1,0:T(8,128)(2,1)} %collective-permute-done.3.refs_5_), channel_id=1, source_target_pairs={{96,0},{112,16},{0,32},{16,48},{32,64},{48,80},{64,96},{80,112},{9... | collective-permute-start | bytes 3538952 | tf_op jit(solution)/shard_map/ppermute | solution.py:56
  114.9 27.2 %collective-permute-start.8 = (bf16[144,4096]{1,0:T(8,128)(2,1)S(1)}, bf16[144,4096]{1,0:T(8,128)(2,1)S(1)}, u32[]{:S(2)}, u32[]{:S(2)}) collective-permute-start(bf16[144,4096]{1,0:T(8,128)(2,1)S(1)} %collective-permute-done.refs_2_), channel_id=1, source_target_pairs={{16,0},{0,16},{48,32},{32,48},{80,64},{64,80},{112,96},{96,112},{1... | collective-permute-start | bytes 3538952 | tf_op jit(solution)/shard_map/ppermute | solution.py:61
  145.9 50.6 %collective-permute-start.28 = (bf16[128,4096]{1,0:T(8,128)(2,1)}, bf16[128,4096]{1,0:T(8,128)(2,1)}, u32[]{:S(2)}, u32[]{:S(2)}) collective-permute-start(bf16[128,4096]{1,0:T(8,128)(2,1)} %copy-done.41), channel_id=1, source_target_pairs={{1,0},{2,1},{3,2},{0,3},{5,4},{6,5},{7,6},{4,7},{9,8},{10,9},{11,1... | collective-permute-start | bytes 3145736 | tf_op jit(solution)/shard_map/ppermute | solution.py:51
  147.4 27.6 %all-to-all-start = ((f32[16,2,128]{2,1,0:T(2,128)}), f32[16,2,128]{2,1,0:T(2,128)S(1)}, u32[]{:S(2)}, u32[]{:S(2)}) async-start(f32[16,2,128]{2,1,0:T(2,128)} %pad_maximum_fusion.2), calls=%async_computation | async-start | bytes 32768 | tf_op jit(solution)/shard_map/all_to_all | solution.py:295
  154.3 40.9 %collective-permute-start.24 = (bf16[64,4096]{1,0:T(8,128)(2,1)}, bf16[64,4096]{1,0:T(8,128)(2,1)}, u32[]{:S(2)}, u32[]{:S(2)}) collective-permute-start(bf16[64,4096]{1,0:T(8,128)(2,1)} %copy-done.24), channel_id=1, source_target_pairs={{12,0},{13,1},{14,2},{15,3},{0,4},{1,5},{2,6},{3,7},{4,8},{5,9},{6... | collective-permute-start | bytes 1572872 | tf_op jit(solution)/shard_map/ppermute | solution.py:51
  156.2 39.4 %collective-permute-start.25 = (bf16[64,4096]{1,0:T(8,128)(2,1)}, bf16[64,4096]{1,0:T(8,128)(2,1)}, u32[]{:S(2)}, u32[]{:S(2)}) collective-permute-start(bf16[64,4096]{1,0:T(8,128)(2,1)} %copy-done.22), channel_id=1, source_target_pairs={{3,0},{0,1},{1,2},{2,3},{7,4},{4,5},{5,6},{6,7},{11,8},{8,9},{9,10... | collective-permute-start | bytes 1572872 | tf_op jit(solution)/shard_map/ppermute | solution.py:51
  157.7 55.7 %collective-permute-start.32 = (bf16[128,4096]{1,0:T(8,128)(2,1)}, bf16[128,4096]{1,0:T(8,128)(2,1)}, u32[]{:S(2)}, u32[]{:S(2)}) collective-permute-start(bf16[128,4096]{1,0:T(8,128)(2,1)} %copy-done.12), channel_id=1, source_target_pairs={{4,0},{5,1},{6,2},{7,3},{8,4},{9,5},{10,6},{11,7},{12,8},{13,9},{1... | collective-permute-start | bytes 3145736 | tf_op jit(solution)/shard_map/ppermute | solution.py:51
  159.4 56.7 %collective-permute-start.33 = (bf16[128,4096]{1,0:T(8,128)(2,1)}, bf16[128,4096]{1,0:T(8,128)(2,1)}, u32[]{:S(2)}, u32[]{:S(2)}) collective-permute-start(bf16[128,4096]{1,0:T(8,128)(2,1)} %copy-done.12), channel_id=1, source_target_pairs={{1,0},{2,1},{3,2},{0,3},{5,4},{6,5},{7,6},{4,7},{9,8},{10,9},{11,1... | collective-permute-start | bytes 3145736 | tf_op jit(solution)/shard_map/ppermute | solution.py:51
  196.5 93.0 %collective-permute-start.50 = (bf16[128,4096]{1,0:T(8,128)(2,1)}, bf16[128,4096]{1,0:T(8,128)(2,1)}, u32[]{:S(2)}, u32[]{:S(2)}) collective-permute-start(bf16[128,4096]{1,0:T(8,128)(2,1)} %get-tuple-element.44), channel_id=1, source_target_pairs={{1,0},{2,1},{3,2},{0,3},{5,4},{6,5},{7,6},{4,7},{9,8},{10,9},{11,1... | collective-permute-start | bytes 3145736 | tf_op jit(solution)/shard_map/ppermute | solution.py:51
  212.7 77.0 %collective-permute-start.49 = (bf16[128,4096]{1,0:T(8,128)(2,1)}, bf16[128,4096]{1,0:T(8,128)(2,1)}, u32[]{:S(2)}, u32[]{:S(2)}) collective-permute-start(bf16[128,4096]{1,0:T(8,128)(2,1)} %get-tuple-element.43), channel_id=1, source_target_pairs={{12,0},{13,1},{14,2},{15,3},{0,4},{1,5},{2,6},{3,7},{4,8},{5,9},{6... | collective-permute-start | bytes 3145736 | tf_op jit(solution)/shard_map/ppermute | solution.py:51
  213.4 97.3 %collective-permute-start.47 = (bf16[128,4096]{1,0:T(8,128)(2,1)S(1)}, bf16[128,4096]{1,0:T(8,128)(2,1)}, u32[]{:S(2)}, u32[]{:S(2)}) collective-permute-start(bf16[128,4096]{1,0:T(8,128)(2,1)S(1)} %get-tuple-element.41), channel_id=1, source_target_pairs={{3,0},{0,1},{1,2},{2,3},{7,4},{4,5},{5,6},{6,7},{11,8},{8,9},{9,10... | collective-permute-start | bytes 3145736 | tf_op jit(solution)/shard_map/ppermute | solution.py:51
  213.4 49.5 %collective-permute-start.39 = (bf16[64,4096]{1,0:T(8,128)(2,1)}, bf16[64,4096]{1,0:T(8,128)(2,1)}, u32[]{:S(2)}, u32[]{:S(2)}) collective-permute-start(bf16[64,4096]{1,0:T(8,128)(2,1)} %get-tuple-element.34), channel_id=1, source_target_pairs={{4,0},{5,1},{6,2},{7,3},{8,4},{9,5},{10,6},{11,7},{12,8},{13,9},{1... | collective-permute-start | bytes 1572872 | tf_op jit(solution)/shard_map/ppermute | solution.py:51
  280.4 27.7 %collective-permute-start.44 = (bf16[128,4096]{1,0:T(8,128)(2,1)S(1)}, bf16[128,4096]{1,0:T(8,128)(2,1)S(1)}, u32[]{:S(2)}, u32[]{:S(2)}) collective-permute-start(bf16[128,4096]{1,0:T(8,128)(2,1)S(1)} %copy-done.19), channel_id=1, source_target_pairs={{3,0},{0,1},{1,2},{2,3},{7,4},{4,5},{5,6},{6,7},{11,8},{8,9},{9,10... | collective-permute-start | bytes 3145736 | tf_op jit(solution)/shard_map/ppermute | solution.py:51
  289.6 35.7 %collective-permute-start.42 = (bf16[128,4096]{1,0:T(8,128)(2,1)S(1)}, bf16[128,4096]{1,0:T(8,128)(2,1)S(1)}, u32[]{:S(2)}, u32[]{:S(2)}) collective-permute-start(bf16[128,4096]{1,0:T(8,128)(2,1)S(1)} %get-tuple-element.36), channel_id=1, source_target_pairs={{3,0},{0,1},{1,2},{2,3},{7,4},{4,5},{5,6},{6,7},{11,8},{8,9},{9,10... | collective-permute-start | bytes 3145736 | tf_op jit(solution)/shard_map/ppermute | solution.py:51
  308.5 40.9 %collective-permute-start.51 = (bf16[128,4096]{1,0:T(8,128)(2,1)S(1)}, bf16[128,4096]{1,0:T(8,128)(2,1)S(1)}, u32[]{:S(2)}, u32[]{:S(2)}) collective-permute-start(bf16[128,4096]{1,0:T(8,128)(2,1)S(1)} %add_convert_fusion.1), channel_id=1, source_target_pairs={{12,0},{13,1},{14,2},{15,3},{0,4},{1,5},{2,6},{3,7},{4,8},{5,9},{6... | collective-permute-start | bytes 3145736 | tf_op jit(solution)/shard_map/ppermute | solution.py:51
  310.7 38.2 %collective-permute-start.45 = (bf16[128,4096]{1,0:T(8,128)(2,1)S(1)}, bf16[128,4096]{1,0:T(8,128)(2,1)S(1)}, u32[]{:S(2)}, u32[]{:S(2)}) collective-permute-start(bf16[128,4096]{1,0:T(8,128)(2,1)S(1)} %add_convert_fusion.4), channel_id=1, source_target_pairs={{12,0},{13,1},{14,2},{15,3},{0,4},{1,5},{2,6},{3,7},{4,8},{5,9},{6... | collective-permute-start | bytes 3145736 | tf_op jit(solution)/shard_map/ppermute | solution.py:51
  313.1 36.3 %collective-permute-start.48 = (bf16[128,4096]{1,0:T(8,128)(2,1)S(1)}, bf16[128,4096]{1,0:T(8,128)(2,1)S(1)}, u32[]{:S(2)}, u32[]{:S(2)}) collective-permute-start(bf16[128,4096]{1,0:T(8,128)(2,1)S(1)} %add_convert_fusion.2), channel_id=1, source_target_pairs={{4,0},{5,1},{6,2},{7,3},{8,4},{9,5},{10,6},{11,7},{12,8},{13,9},{1... | collective-permute-start | bytes 3145736 | tf_op jit(solution)/shard_map/ppermute | solution.py:51
  321.7 27.8 %collective-permute-start.41 = (bf16[128,4096]{1,0:T(8,128)(2,1)S(1)}, bf16[128,4096]{1,0:T(8,128)(2,1)S(1)}, u32[]{:S(2)}, u32[]{:S(2)}) collective-permute-start(bf16[128,4096]{1,0:T(8,128)(2,1)S(1)} %add_convert_fusion.5), channel_id=1, source_target_pairs={{1,0},{2,1},{3,2},{0,3},{5,4},{6,5},{7,6},{4,7},{9,8},{10,9},{11,1... | collective-permute-start | bytes 3145736 | tf_op jit(solution)/shard_map/ppermute | solution.py:51
  (63 other events, 1873.3 us)
